TPU v7x, 512 devices: a whole 4x4x16 slice. The times are simulated.
512 devices in a mesh: leaf: 512 (over y, x, z, core).
Axes of the slice: x: 4, y: 4, z: 16, core: 2. Of those that a mesh axis runs over, the one named last changes fastest.
Arguments:
- vectors: float32 [512, 512, 128], P('leaf'), may hold values from -6 to 6
- points: float32 [512, 3, 512], P('leaf')
- leaf_basis: float32 [512, 512, 128], P('leaf'), may hold values from -0.25 to 0.25
- transfer_leaf: float32 [512, 128, 128], P('leaf'), may hold values from -0.5 to 0.5
- transfer_pair: float32 [32768, 128], P('leaf'), may hold values from -0.5 to 0.5
- transfer_quad: float32 [16384, 128], P('leaf'), may hold values from -0.5 to 0.5
- skel_leaf: float32 [512, 3, 128], P('leaf')
- skel_pair: float32 [256, 3, 128], replicated
- skel_quad: float32 [128, 3, 128], replicated
- skel_top: float32 [64, 3, 128], replicated
- near_list: int32 [512, 16], P('leaf'), may hold values from -1 to 511, as said below
- far_leaf: int32 [512, 8], P('leaf'), may hold values from -1 to 511, as said below
- far_pair: int32 [256, 8], replicated, may hold values from -1 to 255, as said below
- far_quad: int32 [128, 8], replicated, may hold values from -1 to 127, as said below
- far_top: int32 [64, 8], replicated, may hold values from -1 to 63, as said below
Outputs:
- product: float32 [512, 512, 128], P('leaf')
Inputs may be any that keep to these rules, and one draw needn't show every extreme that they name: `near_list`: entry 0 of row l is l; the other entries are distinct leaves within 8 of l, or -1 for an unused slot. `far_leaf`: distinct leaves within 8 of the row's leaf, none of them in that leaf's row of near_list, or -1 for an unused slot. `far_pair`: distinct clusters within 4 of the row's cluster and other than it, or -1 for an unused slot. `far_quad`: distinct clusters within 4 of the row's cluster and other than it, or -1 for an unused slot. `far_top`: distinct top clusters other than the row's cluster, or -1 for an unused slot.
All inputs are finite; a program needn't handle non-finite values.
Results may differ from a plain program's by a relative error of at most 0.0003.
Values sent between devices are 32-bit elements; how exact they have to be, the bound alone decides.
A program may use at most 64 MiB of HBM per device.

v0:
```python
import jax
import jax.numpy as jnp
from jax import lax
from jax.sharding import PartitionSpec as P

REACH = 8
FAR_REACH = 4


INV_FOUR_PI = 0.07957747154594767
DELTA_SQ = 0.01
HIGHEST = lax.Precision.HIGHEST


def from_partner(value, axis, bit):
    mask = 2**bit
    pairs = [(source, source ^ mask) for source in range(lax.axis_size(axis))]
    return lax.ppermute(value, axis, pairs)


def from_behind(block, axis, distance):
    devices = range(lax.axis_size(axis))
    route = [(i - distance, i) for i in devices if i - distance in devices]
    return lax.ppermute(block, axis, route)


def kernel_block(left_pts, right_pts):
    distance = jnp.zeros((left_pts.shape[1], right_pts.shape[1]), jnp.float32)
    for axis_id in range(3):
        offset_gap = left_pts[axis_id][:, None] - right_pts[axis_id][None, :]
        distance = distance + offset_gap * offset_gap
    return INV_FOUR_PI * lax.rsqrt(distance + DELTA_SQ)


def transposed_dot(matrix, values):
    return lax.dot_general(matrix, values, (((0,), (0,)), ((), ())), precision=HIGHEST)


def listed_sum(own_coords, entries, fetcher, width):

    def advance(running, partner):
        coords, values = fetcher(jnp.maximum(partner, 0))
        contrib = jnp.dot(kernel_block(own_coords, coords), values, precision=HIGHEST)
        return (running + jnp.where(partner >= 0, contrib, 0.0), None)

    start_value = jnp.zeros((own_coords.shape[1], width), jnp.float32)
    result, _ = lax.scan(advance, start_value, entries)
    return result


def pair_total(partial_value, levels):
    for bit_index in range(levels):
        partial_value = partial_value + from_partner(partial_value, "leaf", bit_index)
    return partial_value


def join_rows(block, levels, device):
    for bit_index in range(levels):
        other = from_partner(block, "leaf", bit_index)
        upper = device // 2**bit_index % 2
        block = jnp.where(
            upper == 0, jnp.concatenate([block, other], 0), jnp.concatenate([other, block], 0)
        )
    return block


def near_window(shipped):
    gathered = []
    for distance in range(-REACH, REACH + 1):
        if distance == 0:
            gathered.append(shipped)
        else:
            gathered.append(from_behind(shipped, "leaf", -distance))
    return jnp.stack(gathered)


def coef_window(shipped):
    gathered = []
    for distance in range(-REACH, REACH + 1):
        if distance == 0:
            gathered.append(shipped)
        else:
            gathered.append(from_behind(shipped, "leaf", -distance))
    return jnp.stack(gathered)


def partner_stack(coefs, stride):
    gathered = []
    for offset in list(range(-FAR_REACH, 0)) + list(range(1, FAR_REACH + 1)):
        gathered.append(from_behind(coefs, "leaf", -offset * stride))
    stacked = jnp.stack(gathered)

    def slot_of(distance):
        return distance + FAR_REACH - (distance > 0).astype(jnp.int32)

    return (stacked, slot_of)


def middle_level(coefs, skeletons, lists, transfer_rows, above, stride, device):
    width = coefs.shape[1]
    rank_rows = coefs.shape[0] // stride
    cluster = device // stride
    member = device % stride
    own_full = lax.dynamic_index_in_dim(skeletons, cluster, 0, keepdims=False)
    own_coords = lax.dynamic_slice_in_dim(own_full, member * rank_rows, rank_rows, 1)
    stacked, slot_of = partner_stack(coefs, stride)

    def fetcher(partner):
        coords = lax.dynamic_index_in_dim(skeletons, partner, 0, keepdims=False)
        position = jnp.clip(slot_of(partner - cluster), 0, stacked.shape[0] - 1)
        return (coords, lax.dynamic_index_in_dim(stacked, position, 0, keepdims=False))

    entries = lax.dynamic_index_in_dim(lists, cluster, 0, keepdims=False)
    rows_here = listed_sum(own_coords, entries, fetcher, width) + jnp.dot(
        transfer_rows, above, precision=HIGHEST
    )
    return join_rows(rows_here, stride.bit_length() - 1, device)


def per_device(
    vectors,
    points,
    leaf_basis,
    transfer_leaf,
    transfer_pair,
    transfer_quad,
    skel_leaf,
    skel_pair,
    skel_quad,
    skel_top,
    near_list,
    far_leaf,
    far_pair,
    far_quad,
    far_top,
):
    leaf_points = vectors.shape[1]
    width = vectors.shape[2]
    rank = leaf_basis.shape[2]
    device = lax.axis_index("leaf")
    own_points = points[0]
    shipped = jnp.concatenate(
        [vectors[0], own_points.reshape(3 * leaf_points // width, width)], axis=0
    )
    near_rim = near_window(shipped)

    def near_fetch(partner):
        position = jnp.clip(partner - device + REACH, 0, 2 * REACH)
        block = lax.dynamic_index_in_dim(near_rim, position, 0, keepdims=False)
        return (block[leaf_points:].reshape(3, leaf_points), block[:leaf_points])

    near_field = listed_sum(own_points, near_list[0], near_fetch, width)
    coef_leaf = transposed_dot(leaf_basis[0], vectors[0])
    coef_pair = pair_total(transposed_dot(transfer_leaf[0], coef_leaf), 1)
    pair_rows = lax.dynamic_slice_in_dim(coef_pair, device % 2 * (rank // 2), rank // 2, 0)
    coef_quad = pair_total(transposed_dot(transfer_pair, pair_rows), 2)
    quad_rows = lax.dynamic_slice_in_dim(coef_quad, device % 4 * (rank // 4), rank // 4, 0)
    coef_top = pair_total(transposed_dot(transfer_quad, quad_rows), 3)
    top_cluster = device // 8
    top_member = device % 8
    top_rows_own = lax.dynamic_slice_in_dim(coef_top, top_member * (rank // 8), rank // 8, 0)
    top_coords = lax.dynamic_index_in_dim(skel_top, top_cluster, 0, keepdims=False)
    top_entries = lax.dynamic_index_in_dim(far_top, top_cluster, 0, keepdims=False)
    all_top = lax.all_gather(top_rows_own, "leaf", axis=0, tiled=True).reshape(-1, rank, width)

    def top_fetch(partner):
        coords = lax.dynamic_index_in_dim(skel_top, partner, 0, keepdims=False)
        return (coords, lax.dynamic_index_in_dim(all_top, partner, 0, keepdims=False))

    local_top = listed_sum(top_coords, top_entries, top_fetch, width)
    local_quad = middle_level(coef_quad, skel_quad, far_quad, transfer_quad, local_top, 4, device)
    local_pair = middle_level(coef_pair, skel_pair, far_pair, transfer_pair, local_quad, 2, device)
    leaf_ship = jnp.concatenate([coef_leaf, skel_leaf[0]], axis=0)
    leaf_rim = coef_window(leaf_ship)

    def leaf_fetch(partner):
        position = jnp.clip(partner - device + REACH, 0, 2 * REACH)
        block = lax.dynamic_index_in_dim(leaf_rim, position, 0, keepdims=False)
        return (block[rank:], block[:rank])

    local_leaf = listed_sum(skel_leaf[0], far_leaf[0], leaf_fetch, width) + jnp.dot(
        transfer_leaf[0], local_pair, precision=HIGHEST
    )
    product = near_field + jnp.dot(leaf_basis[0], local_leaf, precision=HIGHEST)
    return product[None]


def solution(mesh):
    placed = (
        P("leaf", None, None),
        P("leaf", None, None),
        P("leaf", None, None),
        P("leaf", None, None),
        P("leaf", None),
        P("leaf", None),
        P("leaf", None, None),
        P(),
        P(),
        P(),
        P("leaf", None),
        P("leaf", None),
        P(),
        P(),
        P(),
    )
    return jax.shard_map(
        per_device, mesh=mesh, in_specs=placed, out_specs=P("leaf", None, None), check_vma=False
    )
```

profile of v0, /device:TPU:24, one launch (start us, length us, event | category | flops | bytes accessed | tf_op | source)
XLA Modules:
  0.0 702.0 jit_solution(9183280712991490266)
XLA Ops:
  9.1 9.1 %collective-permute-start.16 = (f32[131,128]{1,0:T(8,128)S(1)}, f32[131,128]{1,0:T(8,128)S(1)}, u32[]{:S(2)}, u32[]{:S(2)}) collective-permute-start(f32[131,128]{1,0:T(8,128)S(1)} %pad_maximum_fusion.1), channel_id=1, source_target_pairs={{0,8},{1,9},{2,10},{3,11},{4,12},{5,13},{6,14},{7,15},{8,16},{9,17... | collective-permute-start | bytes 201224 | tf_op jit(solution)/shard_map/ppermute | solution.py:24
  18.2 5.7 collective-permute-start.17
  23.9 5.9 collective-permute-start.18
  29.8 4.1 collective-permute-start.19
  44.5 3.4 collective-permute-start.20
  51.0 2.6 collective-permute-start.22
  55.9 7.5 %collective-permute-start.24 = (f32[131,128]{1,0:T(8,128)S(1)}, f32[131,128]{1,0:T(8,128)S(1)}, u32[]{:S(2)}, u32[]{:S(2)}) collective-permute-start(f32[131,128]{1,0:T(8,128)S(1)} %pad_maximum_fusion.1), channel_id=1, source_target_pairs={{1,0},{2,1},{3,2},{4,3},{5,4},{6,5},{7,6},{8,7},{9,8},{10,9},{11,1... | collective-permute-start | bytes 201224 | tf_op jit(solution)/shard_map/ppermute | solution.py:24
  63.4 3.3 collective-permute-start.25
  66.7 2.9 collective-permute-start.26
  69.7 4.6 collective-permute-start.27
  74.3 4.1 collective-permute-start.28
  78.4 4.0 collective-permute-start.29
  84.7 5.7 collective-permute-start.31
  90.5 4.0 collective-permute-start
  94.5 4.6 collective-permute-start.1
  99.2 4.8 collective-permute-start.2
  104.0 4.3 collective-permute-start.33
  108.3 4.8 collective-permute-start.34
  114.2 29.7 %while.56 = (s32[]{:T(128)}, f32[128,128]{1,0:T(8,128)S(1)}, s32[8]{0:T(128)S(1)}, f32[3,128]{1,0:T(4,128)S(1)}, s32[]{:T(128)}, /*index=5*/f32[17,131,128]{2,1,...) while((s32[]{:T(128)}, f32[128,128]{1,0:T(8,128)S(1)}, ...), condition=%wide.region_3.4_spmd.clone, body=%wide.region_2.3_spmd.clone.sunk | while | flops 25378828 | bytes 206616 | solution.py:47
  143.9 25.7 %collective-permute-done.33 = f32[128,128]{1,0:T(8,128)S(1)} collective-permute-done((f32[128,128]{1,0:T(8,128)S(1)}, f32[128,128]{1,0:T(8,128)S(1)}, u32[]{:S(2)}, u32[]{:S(2)}) %collective-permute-start.33) | collective-permute-done | bytes 65568 | tf_op jit(solution)/shard_map/ppermute | solution.py:24
  171.5 2.7 collective-permute-start.36
  174.2 6.7 collective-permute-done.35
  182.9 3.8 collective-permute-start.38
  193.7 4.6 collective-permute-start.40
  198.3 2.8 collective-permute-start.42
  201.2 4.1 collective-permute-done.40
  205.3 23.4 %while.57 = (s32[]{:T(128)}, f32[64,128]{1,0:T(8,128)S(1)}, s32[8]{0:T(128)S(1)}, f32[3,64]{1,0:T(4,128)S(1)}, f32[256,3,128]{2,0,1:T(8,128)}, /*index=5*/s32[]{...) while((s32[]{:T(128)}, f32[64,128]{1,0:T(8,128)S(1)}, ...), condition=%wide.region_5.6_spmd.clone, body=%wide.region_4.5_spmd.clone.sunk | while | flops 12689422 | bytes 139043 | solution.py:47
  228.7 7.1 %collective-permute-start.43 = (f32[128,128]{1,0:T(8,128)S(1)}, f32[128,128]{1,0:T(8,128)S(1)}, u32[]{:S(2)}, u32[]{:S(2)}) collective-permute-start(f32[128,128]{1,0:T(8,128)S(1)} %add.194), channel_id=1, source_target_pairs={{0,16},{1,17},{2,18},{3,19},{4,20},{5,21},{6,22},{7,23},{8,24},{9,... | collective-permute-start | bytes 196616 | tf_op jit(solution)/shard_map/ppermute | solution.py:24
  235.8 7.1 %collective-permute-start.44 = (f32[128,128]{1,0:T(8,128)S(1)}, f32[128,128]{1,0:T(8,128)S(1)}, u32[]{:S(2)}, u32[]{:S(2)}) collective-permute-start(f32[128,128]{1,0:T(8,128)S(1)} %add.194), channel_id=1, source_target_pairs={{0,12},{1,13},{2,14},{3,15},{4,16},{5,17},{6,18},{7,19},{8,20},{9,... | collective-permute-start | bytes 196616 | tf_op jit(solution)/shard_map/ppermute | solution.py:24
  243.2 3.8 collective-permute-done.43
  247.0 16.7 %collective-permute-start.45 = (f32[128,128]{1,0:T(8,128)S(1)}, f32[128,128]{1,0:T(8,128)S(1)}, u32[]{:S(2)}, u32[]{:S(2)}) collective-permute-start(f32[128,128]{1,0:T(8,128)S(1)} %add.194), channel_id=1, source_target_pairs={{0,8},{1,9},{2,10},{3,11},{4,12},{5,13},{6,14},{7,15},{8,16},{9,17... | collective-permute-start | bytes 196616 | tf_op jit(solution)/shard_map/ppermute | solution.py:24
  266.0 8.8 %collective-permute-start.47 = (f32[128,128]{1,0:T(8,128)S(1)}, f32[128,128]{1,0:T(8,128)S(1)}, u32[]{:S(2)}, u32[]{:S(2)}) collective-permute-start(f32[128,128]{1,0:T(8,128)S(1)} %add.194), channel_id=1, source_target_pairs={{4,0},{5,1},{6,2},{7,3},{8,4},{9,5},{10,6},{11,7},{12,8},{13,9},{1... | collective-permute-start | bytes 196616 | tf_op jit(solution)/shard_map/ppermute | solution.py:24
  282.3 4.4 collective-permute-done.52
  286.7 5.3 collective-permute-start.3
  292.1 2.9 collective-permute-start.53
  295.0 8.7 %collective-permute-done.53 = f32[128,128]{1,0:T(8,128)S(1)} collective-permute-done((f32[128,128]{1,0:T(8,128)S(1)}, f32[128,128]{1,0:T(8,128)S(1)}, u32[]{:S(2)}, u32[]{:S(2)}) %collective-permute-start.53) | collective-permute-done | bytes 65568 | tf_op jit(solution)/shard_map/ppermute | solution.py:18
  303.6 6.9 collective-permute-start.49
  311.1 5.3 collective-permute-done.49
  316.5 9.5 %collective-permute-start.50 = (f32[128,128]{1,0:T(8,128)S(1)}, f32[128,128]{1,0:T(8,128)S(1)}, u32[]{:S(2)}, u32[]{:S(2)}) collective-permute-start(f32[128,128]{1,0:T(8,128)S(1)} %add.194), channel_id=1, source_target_pairs={{16,0},{17,1},{18,2},{19,3},{20,4},{21,5},{22,6},{23,7},{24,8},{25... | collective-permute-start | bytes 196616 | tf_op jit(solution)/shard_map/ppermute | solution.py:24
  326.0 5.3 collective-permute-done.50
  331.3 7.8 %collective-permute-start.4 = (f32[524,128]{1,0:T(8,128)S(1)}, f32[524,128]{1,0:T(8,128)S(1)}, u32[]{:S(2)}, u32[]{:S(2)}) collective-permute-start(f32[524,128]{1,0:T(8,128)S(1)} %pad_maximum_fusion), channel_id=1, source_target_pairs={{0,4},{1,5},{2,6},{3,7},{4,8},{5,9},{6,10},{7,11},{8,12},{9,13},{1... | collective-permute-start | bytes 804872 | tf_op jit(solution)/shard_map/ppermute | solution.py:24
  339.2 23.4 %while.58 = (s32[]{:T(128)}, f32[32,128]{1,0:T(8,128)S(1)}, s32[8]{0:T(128)S(1)}, f32[3,32]{1,0:T(4,128)S(1)}, f32[128,3,128]{2,0,1:T(8,128)}, /*index=5*/s32[]{...) while((s32[]{:T(128)}, f32[32,128]{1,0:T(8,128)S(1)}, ...), condition=%wide.region_7.8_spmd.clone, body=%wide.region_6.7_spmd.clone.sunk | while | flops 6344718 | bytes 105507 | solution.py:47
  362.6 8.1 %collective-permute-start.5 = (f32[524,128]{1,0:T(8,128)S(1)}, f32[524,128]{1,0:T(8,128)S(1)}, u32[]{:S(2)}, u32[]{:S(2)}) collective-permute-start(f32[524,128]{1,0:T(8,128)S(1)} %pad_maximum_fusion), channel_id=1, source_target_pairs={{0,3},{1,4},{2,5},{3,6},{4,7},{5,8},{6,9},{7,10},{8,11},{9,12},{10... | collective-permute-start | bytes 804872 | tf_op jit(solution)/shard_map/ppermute | solution.py:24
  371.3 2.4 collective-permute-start.6
  377.1 7.8 %collective-permute-start.8 = (f32[524,128]{1,0:T(8,128)S(1)}, f32[524,128]{1,0:T(8,128)S(1)}, u32[]{:S(2)}, u32[]{:S(2)}) collective-permute-start(f32[524,128]{1,0:T(8,128)S(1)} %pad_maximum_fusion), channel_id=1, source_target_pairs={{1,0},{2,1},{3,2},{4,3},{5,4},{6,5},{7,6},{8,7},{9,8},{10,9},{11,1... | collective-permute-start | bytes 804872 | tf_op jit(solution)/shard_map/ppermute | solution.py:24
  385.7 3.4 collective-permute-start.9
  389.9 3.1 collective-permute-start.10
  393.7 3.5 collective-permute-start.11
  401.3 2.4 collective-permute-start.13
  407.3 3.2 collective-permute-done.10
  410.5 8.0 %collective-permute-start.15 = (f32[524,128]{1,0:T(8,128)S(1)}, f32[524,128]{1,0:T(8,128)S(1)}, u32[]{:S(2)}, u32[]{:S(2)}) collective-permute-start(f32[524,128]{1,0:T(8,128)S(1)} %pad_maximum_fusion), channel_id=1, source_target_pairs={{8,0},{9,1},{10,2},{11,3},{12,4},{13,5},{14,6},{15,7},{16,8},{17,9... | collective-permute-start | bytes 804872 | tf_op jit(solution)/shard_map/ppermute | solution.py:24
  420.0 17.4 %collective-permute-done.12 = f32[524,128]{1,0:T(8,128)S(1)} collective-permute-done((f32[524,128]{1,0:T(8,128)S(1)}, f32[524,128]{1,0:T(8,128)S(1)}, u32[]{:S(2)}, u32[]{:S(2)}) %collective-permute-start.12) | collective-permute-done | bytes 268320 | tf_op jit(solution)/shard_map/ppermute | solution.py:24
  438.2 11.9 %collective-permute-done.13 = f32[524,128]{1,0:T(8,128)S(1)} collective-permute-done((f32[524,128]{1,0:T(8,128)S(1)}, f32[524,128]{1,0:T(8,128)S(1)}, u32[]{:S(2)}, u32[]{:S(2)}) %collective-permute-start.13) | collective-permute-done | bytes 268320 | tf_op jit(solution)/shard_map/ppermute | solution.py:24
  450.8 120.0 %all-gather.2.cloned.1.call-done = f32[8192,128]{1,0:T(8,128)} async-done(((f32[16,128]{1,0:T(8,128)}), f32[8192,128]{1,0:T(8,128)}) %all-gather.2.cloned.1.call-update) | async-done | bytes 4194320 | tf_op jit(solution)/shard_map/all_gather | solution.py:164
  570.8 30.4 %while.59 = (s32[]{:T(128)}, f32[128,128]{1,0:T(8,128)S(1)}, s32[8]{0:T(128)S(1)}, f32[3,128]{1,0:T(4,128)S(1)}, f32[64,3,128]{2,0,1:T(8,128)}, /*index=5*/f32[6...) while((s32[]{:T(128)}, f32[128,128]{1,0:T(8,128)S(1)}, ...), condition=%wide.region_9.10_spmd.clone, body=%wide.region_8.9_spmd.clone.sunk | while | flops 25378824 | bytes 207036 | solution.py:47
  604.5 3.4 collective-permute-start.55
  612.5 81.0 %while.55 = (s32[]{:T(128)}, f32[512,128]{1,0:T(8,128)S(1)}, s32[16]{0:T(128)S(1)}, f32[3,512]{1,0:T(4,128)S(1)}, s32[]{:T(128)}, /*index=5*/f32[17,524,128]{2,1...) while((s32[]{:T(128)}, f32[512,128]{1,0:T(8,128)S(1)}, ...), condition=%wide.region_1.2_spmd.clone, body=%wide.region_0.1_spmd.clone.sunk | while | flops 405471232 | bytes 824088 | solution.py:47
  615.2 2.4 fusion.187
  620.3 2.4 fusion.187
  625.3 2.4 fusion.187
  630.4 2.4 fusion.187
  635.5 2.4 fusion.187
  665.8 2.4 fusion.187
  675.9 2.4 fusion.187
  (355 shorter events, 177.8 us)
Async XLA Ops:
  6.5 107.6 %copy-start.6 = (s32[1,8]{1,0:T(1,128)S(1)}, s32[1,8]{1,0:T(1,128)}, u32[]{:S(2)}) copy-start(s32[1,8]{1,0:T(1,128)} %param.36) | copy-start | bytes 100
  6.5 564.3 %all-gather.2.cloned.1.call-start = ((), (), s32[]{:S(2)}) async-start(), calls=%async_computation | async-start | bytes 4202496 | tf_op jit(solution)/shard_map/all_gather | solution.py:164
  9.1 40.0 %collective-permute-start.16 = (f32[131,128]{1,0:T(8,128)S(1)}, f32[131,128]{1,0:T(8,128)S(1)}, u32[]{:S(2)}, u32[]{:S(2)}) collective-permute-start(f32[131,128]{1,0:T(8,128)S(1)} %pad_maximum_fusion.1), channel_id=1, source_target_pairs={{0,8},{1,9},{2,10},{3,11},{4,12},{5,13},{6,14},{7,15},{8,16},{9,17... | collective-permute-start | bytes 201224 | tf_op jit(solution)/shard_map/ppermute | solution.py:24
  18.2 32.8 %collective-permute-start.17 = (f32[131,128]{1,0:T(8,128)S(1)}, f32[131,128]{1,0:T(8,128)S(1)}, u32[]{:S(2)}, u32[]{:S(2)}) collective-permute-start(f32[131,128]{1,0:T(8,128)S(1)} %pad_maximum_fusion.1), channel_id=1, source_target_pairs={{0,7},{1,8},{2,9},{3,10},{4,11},{5,12},{6,13},{7,14},{8,15},{9,16}... | collective-permute-start | bytes 201224 | tf_op jit(solution)/shard_map/ppermute | solution.py:24
  23.9 29.7 %collective-permute-start.18 = (f32[131,128]{1,0:T(8,128)S(1)}, f32[131,128]{1,0:T(8,128)S(1)}, u32[]{:S(2)}, u32[]{:S(2)}) collective-permute-start(f32[131,128]{1,0:T(8,128)S(1)} %pad_maximum_fusion.1), channel_id=1, source_target_pairs={{0,6},{1,7},{2,8},{3,9},{4,10},{5,11},{6,12},{7,13},{8,14},{9,15},... | collective-permute-start | bytes 201224 | tf_op jit(solution)/shard_map/ppermute | solution.py:24
  29.8 26.1 %collective-permute-start.19 = (f32[131,128]{1,0:T(8,128)S(1)}, f32[131,128]{1,0:T(8,128)S(1)}, u32[]{:S(2)}, u32[]{:S(2)}) collective-permute-start(f32[131,128]{1,0:T(8,128)S(1)} %pad_maximum_fusion.1), channel_id=1, source_target_pairs={{0,5},{1,6},{2,7},{3,8},{4,9},{5,10},{6,11},{7,12},{8,13},{9,14},{... | collective-permute-start | bytes 201224 | tf_op jit(solution)/shard_map/ppermute | solution.py:24
  35.1 9.5 %collective-permute-start.32 = (f32[128,128]{1,0:T(8,128)S(1)}, f32[128,128]{1,0:T(8,128)S(1)}, u32[]{:S(2)}, u32[]{:S(2)}) collective-permute-start(f32[128,128]{1,0:T(8,128)S(1)} %convolution_bitcast_fusion.4), channel_id=1, source_target_pairs={{0,1},{1,0},{2,3},{3,2},{4,5},{5,4},{6,7},{7,6},{8,9},{9,8},{10,11... | collective-permute-start | bytes 196616 | tf_op jit(solution)/shard_map/ppermute | solution.py:18
  37.1 205.9 %copy-start.4 = (f32[32,128]{1,0:T(8,128)S(1)}, f32[32,128]{1,0:T(8,128)}, u32[]{:S(2)}) copy-start(f32[32,128]{1,0:T(8,128)} %param.30) | copy-start | bytes 49156
  44.5 18.9 %collective-permute-start.20 = (f32[131,128]{1,0:T(8,128)S(1)}, f32[131,128]{1,0:T(8,128)S(1)}, u32[]{:S(2)}, u32[]{:S(2)}) collective-permute-start(f32[131,128]{1,0:T(8,128)S(1)} %pad_maximum_fusion.1), channel_id=1, source_target_pairs={{0,4},{1,5},{2,6},{3,7},{4,8},{5,9},{6,10},{7,11},{8,12},{9,13},{1... | collective-permute-start | bytes 201224 | tf_op jit(solution)/shard_map/ppermute | solution.py:24
  49.0 17.7 %collective-permute-start.21 = (f32[131,128]{1,0:T(8,128)S(1)}, f32[131,128]{1,0:T(8,128)S(1)}, u32[]{:S(2)}, u32[]{:S(2)}) collective-permute-start(f32[131,128]{1,0:T(8,128)S(1)} %pad_maximum_fusion.1), channel_id=1, source_target_pairs={{0,3},{1,4},{2,5},{3,6},{4,7},{5,8},{6,9},{7,10},{8,11},{9,12},{10... | collective-permute-start | bytes 201224 | tf_op jit(solution)/shard_map/ppermute | solution.py:24
  51.0 18.7 %collective-permute-start.22 = (f32[131,128]{1,0:T(8,128)S(1)}, f32[131,128]{1,0:T(8,128)S(1)}, u32[]{:S(2)}, u32[]{:S(2)}) collective-permute-start(f32[131,128]{1,0:T(8,128)S(1)} %pad_maximum_fusion.1), channel_id=1, source_target_pairs={{0,2},{1,3},{2,4},{3,5},{4,6},{5,7},{6,8},{7,9},{8,10},{9,11},{10,... | collective-permute-start | bytes 201224 | tf_op jit(solution)/shard_map/ppermute | solution.py:24
  53.6 20.7 %collective-permute-start.23 = (f32[131,128]{1,0:T(8,128)S(1)}, f32[131,128]{1,0:T(8,128)S(1)}, u32[]{:S(2)}, u32[]{:S(2)}) collective-permute-start(f32[131,128]{1,0:T(8,128)S(1)} %pad_maximum_fusion.1), channel_id=1, source_target_pairs={{0,1},{1,2},{2,3},{3,4},{4,5},{5,6},{6,7},{7,8},{8,9},{9,10},{10,1... | collective-permute-start | bytes 201224 | tf_op jit(solution)/shard_map/ppermute | solution.py:24
  55.9 22.5 %collective-permute-start.24 = (f32[131,128]{1,0:T(8,128)S(1)}, f32[131,128]{1,0:T(8,128)S(1)}, u32[]{:S(2)}, u32[]{:S(2)}) collective-permute-start(f32[131,128]{1,0:T(8,128)S(1)} %pad_maximum_fusion.1), channel_id=1, source_target_pairs={{1,0},{2,1},{3,2},{4,3},{5,4},{6,5},{7,6},{8,7},{9,8},{10,9},{11,1... | collective-permute-start | bytes 201224 | tf_op jit(solution)/shard_map/ppermute | solution.py:24
  63.4 19.0 %collective-permute-start.25 = (f32[131,128]{1,0:T(8,128)S(1)}, f32[131,128]{1,0:T(8,128)S(1)}, u32[]{:S(2)}, u32[]{:S(2)}) collective-permute-start(f32[131,128]{1,0:T(8,128)S(1)} %pad_maximum_fusion.1), channel_id=1, source_target_pairs={{2,0},{3,1},{4,2},{5,3},{6,4},{7,5},{8,6},{9,7},{10,8},{11,9},{12,... | collective-permute-start | bytes 201224 | tf_op jit(solution)/shard_map/ppermute | solution.py:24
  66.7 18.0 %collective-permute-start.26 = (f32[131,128]{1,0:T(8,128)S(1)}, f32[131,128]{1,0:T(8,128)S(1)}, u32[]{:S(2)}, u32[]{:S(2)}) collective-permute-start(f32[131,128]{1,0:T(8,128)S(1)} %pad_maximum_fusion.1), channel_id=1, source_target_pairs={{3,0},{4,1},{5,2},{6,3},{7,4},{8,5},{9,6},{10,7},{11,8},{12,9},{13... | collective-permute-start | bytes 201224 | tf_op jit(solution)/shard_map/ppermute | solution.py:24
  69.7 20.8 %collective-permute-start.27 = (f32[131,128]{1,0:T(8,128)S(1)}, f32[131,128]{1,0:T(8,128)S(1)}, u32[]{:S(2)}, u32[]{:S(2)}) collective-permute-start(f32[131,128]{1,0:T(8,128)S(1)} %pad_maximum_fusion.1), channel_id=1, source_target_pairs={{4,0},{5,1},{6,2},{7,3},{8,4},{9,5},{10,6},{11,7},{12,8},{13,9},{1... | collective-permute-start | bytes 201224 | tf_op jit(solution)/shard_map/ppermute | solution.py:24
  74.3 20.2 %collective-permute-start.28 = (f32[131,128]{1,0:T(8,128)S(1)}, f32[131,128]{1,0:T(8,128)S(1)}, u32[]{:S(2)}, u32[]{:S(2)}) collective-permute-start(f32[131,128]{1,0:T(8,128)S(1)} %pad_maximum_fusion.1), channel_id=1, source_target_pairs={{5,0},{6,1},{7,2},{8,3},{9,4},{10,5},{11,6},{12,7},{13,8},{14,9},{... | collective-permute-start | bytes 201224 | tf_op jit(solution)/shard_map/ppermute | solution.py:24
  78.4 20.7 %collective-permute-start.29 = (f32[131,128]{1,0:T(8,128)S(1)}, f32[131,128]{1,0:T(8,128)S(1)}, u32[]{:S(2)}, u32[]{:S(2)}) collective-permute-start(f32[131,128]{1,0:T(8,128)S(1)} %pad_maximum_fusion.1), channel_id=1, source_target_pairs={{6,0},{7,1},{8,2},{9,3},{10,4},{11,5},{12,6},{13,7},{14,8},{15,9},... | collective-permute-start | bytes 201224 | tf_op jit(solution)/shard_map/ppermute | solution.py:24
  82.5 21.5 %collective-permute-start.30 = (f32[131,128]{1,0:T(8,128)S(1)}, f32[131,128]{1,0:T(8,128)S(1)}, u32[]{:S(2)}, u32[]{:S(2)}) collective-permute-start(f32[131,128]{1,0:T(8,128)S(1)} %pad_maximum_fusion.1), channel_id=1, source_target_pairs={{7,0},{8,1},{9,2},{10,3},{11,4},{12,5},{13,6},{14,7},{15,8},{16,9}... | collective-permute-start | bytes 201224 | tf_op jit(solution)/shard_map/ppermute | solution.py:24
  84.7 23.6 %collective-permute-start.31 = (f32[131,128]{1,0:T(8,128)S(1)}, f32[131,128]{1,0:T(8,128)S(1)}, u32[]{:S(2)}, u32[]{:S(2)}) collective-permute-start(f32[131,128]{1,0:T(8,128)S(1)} %pad_maximum_fusion.1), channel_id=1, source_target_pairs={{8,0},{9,1},{10,2},{11,3},{12,4},{13,5},{14,6},{15,7},{16,8},{17,9... | collective-permute-start | bytes 201224 | tf_op jit(solution)/shard_map/ppermute | solution.py:24
  90.5 272.1 %collective-permute-start = (f32[524,128]{1,0:T(8,128)S(1)}, f32[524,128]{1,0:T(8,128)S(1)}, u32[]{:S(2)}, u32[]{:S(2)}) collective-permute-start(f32[524,128]{1,0:T(8,128)S(1)} %pad_maximum_fusion), channel_id=1, source_target_pairs={{0,8},{1,9},{2,10},{3,11},{4,12},{5,13},{6,14},{7,15},{8,16},{9,17... | collective-permute-start | bytes 804872 | tf_op jit(solution)/shard_map/ppermute | solution.py:24
  94.5 276.8 %collective-permute-start.1 = (f32[524,128]{1,0:T(8,128)S(1)}, f32[524,128]{1,0:T(8,128)S(1)}, u32[]{:S(2)}, u32[]{:S(2)}) collective-permute-start(f32[524,128]{1,0:T(8,128)S(1)} %pad_maximum_fusion), channel_id=1, source_target_pairs={{0,7},{1,8},{2,9},{3,10},{4,11},{5,12},{6,13},{7,14},{8,15},{9,16}... | collective-permute-start | bytes 804872 | tf_op jit(solution)/shard_map/ppermute | solution.py:24
  99.2 275.4 %collective-permute-start.2 = (f32[524,128]{1,0:T(8,128)S(1)}, f32[524,128]{1,0:T(8,128)S(1)}, u32[]{:S(2)}, u32[]{:S(2)}) collective-permute-start(f32[524,128]{1,0:T(8,128)S(1)} %pad_maximum_fusion), channel_id=1, source_target_pairs={{0,6},{1,7},{2,8},{3,9},{4,10},{5,11},{6,12},{7,13},{8,14},{9,15},... | collective-permute-start | bytes 804872 | tf_op jit(solution)/shard_map/ppermute | solution.py:24
  104.0 65.6 %collective-permute-start.33 = (f32[128,128]{1,0:T(8,128)S(1)}, f32[128,128]{1,0:T(8,128)S(1)}, u32[]{:S(2)}, u32[]{:S(2)}) collective-permute-start(f32[128,128]{1,0:T(8,128)S(1)} %add.188), channel_id=1, source_target_pairs={{0,8},{1,9},{2,10},{3,11},{4,12},{5,13},{6,14},{7,15},{8,16},{9,17... | collective-permute-start | bytes 196616 | tf_op jit(solution)/shard_map/ppermute | solution.py:24
  108.3 63.2 %collective-permute-start.34 = (f32[128,128]{1,0:T(8,128)S(1)}, f32[128,128]{1,0:T(8,128)S(1)}, u32[]{:S(2)}, u32[]{:S(2)}) collective-permute-start(f32[128,128]{1,0:T(8,128)S(1)} %add.188), channel_id=1, source_target_pairs={{0,6},{1,7},{2,8},{3,9},{4,10},{5,11},{6,12},{7,13},{8,14},{9,15},... | collective-permute-start | bytes 196616 | tf_op jit(solution)/shard_map/ppermute | solution.py:24
  169.6 11.4 %collective-permute-start.35 = (f32[128,128]{1,0:T(8,128)S(1)}, f32[128,128]{1,0:T(8,128)S(1)}, u32[]{:S(2)}, u32[]{:S(2)}) collective-permute-start(f32[128,128]{1,0:T(8,128)S(1)} %add.188), channel_id=1, source_target_pairs={{0,4},{1,5},{2,6},{3,7},{4,8},{5,9},{6,10},{7,11},{8,12},{9,13},{1... | collective-permute-start | bytes 196616 | tf_op jit(solution)/shard_map/ppermute | solution.py:24
  171.5 11.4 %collective-permute-start.36 = (f32[128,128]{1,0:T(8,128)S(1)}, f32[128,128]{1,0:T(8,128)S(1)}, u32[]{:S(2)}, u32[]{:S(2)}) collective-permute-start(f32[128,128]{1,0:T(8,128)S(1)} %add.188), channel_id=1, source_target_pairs={{0,2},{1,3},{2,4},{3,5},{4,6},{5,7},{6,8},{7,9},{8,10},{9,11},{10,... | collective-permute-start | bytes 196616 | tf_op jit(solution)/shard_map/ppermute | solution.py:24
  181.0 7.5 %collective-permute-start.37 = (f32[128,128]{1,0:T(8,128)S(1)}, f32[128,128]{1,0:T(8,128)S(1)}, u32[]{:S(2)}, u32[]{:S(2)}) collective-permute-start(f32[128,128]{1,0:T(8,128)S(1)} %add.188), channel_id=1, source_target_pairs={{2,0},{3,1},{4,2},{5,3},{6,4},{7,5},{8,6},{9,7},{10,8},{11,9},{12,... | collective-permute-start | bytes 196616 | tf_op jit(solution)/shard_map/ppermute | solution.py:24
  182.9 7.6 %collective-permute-start.38 = (f32[128,128]{1,0:T(8,128)S(1)}, f32[128,128]{1,0:T(8,128)S(1)}, u32[]{:S(2)}, u32[]{:S(2)}) collective-permute-start(f32[128,128]{1,0:T(8,128)S(1)} %add.188), channel_id=1, source_target_pairs={{4,0},{5,1},{6,2},{7,3},{8,4},{9,5},{10,6},{11,7},{12,8},{13,9},{1... | collective-permute-start | bytes 196616 | tf_op jit(solution)/shard_map/ppermute | solution.py:24
  188.5 9.8 %collective-permute-start.39 = (f32[128,128]{1,0:T(8,128)S(1)}, f32[128,128]{1,0:T(8,128)S(1)}, u32[]{:S(2)}, u32[]{:S(2)}) collective-permute-start(f32[128,128]{1,0:T(8,128)S(1)} %add.188), channel_id=1, source_target_pairs={{6,0},{7,1},{8,2},{9,3},{10,4},{11,5},{12,6},{13,7},{14,8},{15,9},... | collective-permute-start | bytes 196616 | tf_op jit(solution)/shard_map/ppermute | solution.py:24
  190.5 3.1 collective-permute-start.41
  193.7 11.6 %collective-permute-start.40 = (f32[128,128]{1,0:T(8,128)S(1)}, f32[128,128]{1,0:T(8,128)S(1)}, u32[]{:S(2)}, u32[]{:S(2)}) collective-permute-start(f32[128,128]{1,0:T(8,128)S(1)} %add.188), channel_id=1, source_target_pairs={{8,0},{9,1},{10,2},{11,3},{12,4},{13,5},{14,6},{15,7},{16,8},{17,9... | collective-permute-start | bytes 196616 | tf_op jit(solution)/shard_map/ppermute | solution.py:24
  198.3 30.4 %collective-permute-start.42 = (f32[128,128]{1,0:T(8,128)S(1)}, f32[128,128]{1,0:T(8,128)S(1)}, u32[]{:S(2)}, u32[]{:S(2)}) collective-permute-start(f32[128,128]{1,0:T(8,128)S(1)} %add.193), channel_id=1, source_target_pairs={{0,2},{1,3},{2,0},{3,1},{4,6},{5,7},{6,4},{7,5},{8,10},{9,11},{10,... | collective-permute-start | bytes 196616 | tf_op jit(solution)/shard_map/ppermute | solution.py:18
  205.3 195.3 %copy-start.1 = (f32[1,512,128]{2,1,0:T(8,128)S(1)}, f32[1,512,128]{2,1,0:T(8,128)}, u32[]{:S(2)}) copy-start(f32[1,512,128]{2,1,0:T(8,128)} %param.25) | copy-start | bytes 786436
  228.7 18.3 %collective-permute-start.43 = (f32[128,128]{1,0:T(8,128)S(1)}, f32[128,128]{1,0:T(8,128)S(1)}, u32[]{:S(2)}, u32[]{:S(2)}) collective-permute-start(f32[128,128]{1,0:T(8,128)S(1)} %add.194), channel_id=1, source_target_pairs={{0,16},{1,17},{2,18},{3,19},{4,20},{5,21},{6,22},{7,23},{8,24},{9,... | collective-permute-start | bytes 196616 | tf_op jit(solution)/shard_map/ppermute | solution.py:24
  235.8 27.9 %collective-permute-start.44 = (f32[128,128]{1,0:T(8,128)S(1)}, f32[128,128]{1,0:T(8,128)S(1)}, u32[]{:S(2)}, u32[]{:S(2)}) collective-permute-start(f32[128,128]{1,0:T(8,128)S(1)} %add.194), channel_id=1, source_target_pairs={{0,12},{1,13},{2,14},{3,15},{4,16},{5,17},{6,18},{7,19},{8,20},{9,... | collective-permute-start | bytes 196616 | tf_op jit(solution)/shard_map/ppermute | solution.py:24
  247.0 18.9 %collective-permute-start.45 = (f32[128,128]{1,0:T(8,128)S(1)}, f32[128,128]{1,0:T(8,128)S(1)}, u32[]{:S(2)}, u32[]{:S(2)}) collective-permute-start(f32[128,128]{1,0:T(8,128)S(1)} %add.194), channel_id=1, source_target_pairs={{0,8},{1,9},{2,10},{3,11},{4,12},{5,13},{6,14},{7,15},{8,16},{9,17... | collective-permute-start | bytes 196616 | tf_op jit(solution)/shard_map/ppermute | solution.py:24
  263.8 11.3 %collective-permute-start.46 = (f32[128,128]{1,0:T(8,128)S(1)}, f32[128,128]{1,0:T(8,128)S(1)}, u32[]{:S(2)}, u32[]{:S(2)}) collective-permute-start(f32[128,128]{1,0:T(8,128)S(1)} %add.194), channel_id=1, source_target_pairs={{0,4},{1,5},{2,6},{3,7},{4,8},{5,9},{6,10},{7,11},{8,12},{9,13},{1... | collective-permute-start | bytes 196616 | tf_op jit(solution)/shard_map/ppermute | solution.py:24
  266.0 14.1 %collective-permute-start.47 = (f32[128,128]{1,0:T(8,128)S(1)}, f32[128,128]{1,0:T(8,128)S(1)}, u32[]{:S(2)}, u32[]{:S(2)}) collective-permute-start(f32[128,128]{1,0:T(8,128)S(1)} %add.194), channel_id=1, source_target_pairs={{4,0},{5,1},{6,2},{7,3},{8,4},{9,5},{10,6},{11,7},{12,8},{13,9},{1... | collective-permute-start | bytes 196616 | tf_op jit(solution)/shard_map/ppermute | solution.py:24
  275.0 3.1 collective-permute-start.51
  278.2 13.9 %collective-permute-start.48 = (f32[128,128]{1,0:T(8,128)S(1)}, f32[128,128]{1,0:T(8,128)S(1)}, u32[]{:S(2)}, u32[]{:S(2)}) collective-permute-start(f32[128,128]{1,0:T(8,128)S(1)} %add.194), channel_id=1, source_target_pairs={{8,0},{9,1},{10,2},{11,3},{12,4},{13,5},{14,6},{15,7},{16,8},{17,9... | collective-permute-start | bytes 196616 | tf_op jit(solution)/shard_map/ppermute | solution.py:24
  280.1 6.6 collective-permute-start.52
  286.7 90.4 %collective-permute-start.3 = (f32[524,128]{1,0:T(8,128)S(1)}, f32[524,128]{1,0:T(8,128)S(1)}, u32[]{:S(2)}, u32[]{:S(2)}) collective-permute-start(f32[524,128]{1,0:T(8,128)S(1)} %pad_maximum_fusion), channel_id=1, source_target_pairs={{0,5},{1,6},{2,7},{3,8},{4,9},{5,10},{6,11},{7,12},{8,13},{9,14},{... | collective-permute-start | bytes 804872 | tf_op jit(solution)/shard_map/ppermute | solution.py:24
  292.1 11.6 %collective-permute-start.53 = (f32[128,128]{1,0:T(8,128)S(1)}, f32[128,128]{1,0:T(8,128)S(1)}, u32[]{:S(2)}, u32[]{:S(2)}) collective-permute-start(f32[128,128]{1,0:T(8,128)S(1)} %add.197), channel_id=1, source_target_pairs={{0,4},{1,5},{2,6},{3,7},{4,0},{5,1},{6,2},{7,3},{8,12},{9,13},{10,... | collective-permute-start | bytes 196616 | tf_op jit(solution)/shard_map/ppermute | solution.py:18
  303.6 12.8 %collective-permute-start.49 = (f32[128,128]{1,0:T(8,128)S(1)}, f32[128,128]{1,0:T(8,128)S(1)}, u32[]{:S(2)}, u32[]{:S(2)}) collective-permute-start(f32[128,128]{1,0:T(8,128)S(1)} %add.194), channel_id=1, source_target_pairs={{12,0},{13,1},{14,2},{15,3},{16,4},{17,5},{18,6},{19,7},{20,8},{21... | collective-permute-start | bytes 196616 | tf_op jit(solution)/shard_map/ppermute | solution.py:24
  316.5 14.9 %collective-permute-start.50 = (f32[128,128]{1,0:T(8,128)S(1)}, f32[128,128]{1,0:T(8,128)S(1)}, u32[]{:S(2)}, u32[]{:S(2)}) collective-permute-start(f32[128,128]{1,0:T(8,128)S(1)} %add.194), channel_id=1, source_target_pairs={{16,0},{17,1},{18,2},{19,3},{20,4},{21,5},{22,6},{23,7},{24,8},{25... | collective-permute-start | bytes 196616 | tf_op jit(solution)/shard_map/ppermute | solution.py:24
  331.3 54.4 %collective-permute-start.4 = (f32[524,128]{1,0:T(8,128)S(1)}, f32[524,128]{1,0:T(8,128)S(1)}, u32[]{:S(2)}, u32[]{:S(2)}) collective-permute-start(f32[524,128]{1,0:T(8,128)S(1)} %pad_maximum_fusion), channel_id=1, source_target_pairs={{0,4},{1,5},{2,6},{3,7},{4,8},{5,9},{6,10},{7,11},{8,12},{9,13},{1... | collective-permute-start | bytes 804872 | tf_op jit(solution)/shard_map/ppermute | solution.py:24
  362.6 27.3 %collective-permute-start.5 = (f32[524,128]{1,0:T(8,128)S(1)}, f32[524,128]{1,0:T(8,128)S(1)}, u32[]{:S(2)}, u32[]{:S(2)}) collective-permute-start(f32[524,128]{1,0:T(8,128)S(1)} %pad_maximum_fusion), channel_id=1, source_target_pairs={{0,3},{1,4},{2,5},{3,6},{4,7},{5,8},{6,9},{7,10},{8,11},{9,12},{10... | collective-permute-start | bytes 804872 | tf_op jit(solution)/shard_map/ppermute | solution.py:24
  371.3 22.3 %collective-permute-start.6 = (f32[524,128]{1,0:T(8,128)S(1)}, f32[524,128]{1,0:T(8,128)S(1)}, u32[]{:S(2)}, u32[]{:S(2)}) collective-permute-start(f32[524,128]{1,0:T(8,128)S(1)} %pad_maximum_fusion), channel_id=1, source_target_pairs={{0,2},{1,3},{2,4},{3,5},{4,6},{5,7},{6,8},{7,9},{8,10},{9,11},{10,... | collective-permute-start | bytes 804872 | tf_op jit(solution)/shard_map/ppermute | solution.py:24
  374.5 23.4 %collective-permute-start.7 = (f32[524,128]{1,0:T(8,128)S(1)}, f32[524,128]{1,0:T(8,128)S(1)}, u32[]{:S(2)}, u32[]{:S(2)}) collective-permute-start(f32[524,128]{1,0:T(8,128)S(1)} %pad_maximum_fusion), channel_id=1, source_target_pairs={{0,1},{1,2},{2,3},{3,4},{4,5},{5,6},{6,7},{7,8},{8,9},{9,10},{10,1... | collective-permute-start | bytes 804872 | tf_op jit(solution)/shard_map/ppermute | solution.py:24
  377.1 24.1 %collective-permute-start.8 = (f32[524,128]{1,0:T(8,128)S(1)}, f32[524,128]{1,0:T(8,128)S(1)}, u32[]{:S(2)}, u32[]{:S(2)}) collective-permute-start(f32[524,128]{1,0:T(8,128)S(1)} %pad_maximum_fusion), channel_id=1, source_target_pairs={{1,0},{2,1},{3,2},{4,3},{5,4},{6,5},{7,6},{8,7},{9,8},{10,9},{11,1... | collective-permute-start | bytes 804872 | tf_op jit(solution)/shard_map/ppermute | solution.py:24
  385.7 18.7 %collective-permute-start.9 = (f32[524,128]{1,0:T(8,128)S(1)}, f32[524,128]{1,0:T(8,128)S(1)}, u32[]{:S(2)}, u32[]{:S(2)}) collective-permute-start(f32[524,128]{1,0:T(8,128)S(1)} %pad_maximum_fusion), channel_id=1, source_target_pairs={{2,0},{3,1},{4,2},{5,3},{6,4},{7,5},{8,6},{9,7},{10,8},{11,9},{12,... | collective-permute-start | bytes 804872 | tf_op jit(solution)/shard_map/ppermute | solution.py:24
  389.9 20.7 %collective-permute-start.10 = (f32[524,128]{1,0:T(8,128)S(1)}, f32[524,128]{1,0:T(8,128)S(1)}, u32[]{:S(2)}, u32[]{:S(2)}) collective-permute-start(f32[524,128]{1,0:T(8,128)S(1)} %pad_maximum_fusion), channel_id=1, source_target_pairs={{3,0},{4,1},{5,2},{6,3},{7,4},{8,5},{9,6},{10,7},{11,8},{12,9},{13... | collective-permute-start | bytes 804872 | tf_op jit(solution)/shard_map/ppermute | solution.py:24
  393.7 216.7 %copy-start.3 = (f32[64,128]{1,0:T(8,128)S(1)}, f32[64,128]{1,0:T(8,128)}, u32[]{:S(2)}) copy-start(f32[64,128]{1,0:T(8,128)} %param.29) | copy-start | bytes 98308
  393.7 218.8 %copy-start.7 = (s32[1,16]{1,0:T(1,128)S(1)}, s32[1,16]{1,0:T(1,128)}, u32[]{:S(2)}) copy-start(s32[1,16]{1,0:T(1,128)} %param.35) | copy-start | bytes 196
  393.7 25.6 %collective-permute-start.11 = (f32[524,128]{1,0:T(8,128)S(1)}, f32[524,128]{1,0:T(8,128)S(1)}, u32[]{:S(2)}, u32[]{:S(2)}) collective-permute-start(f32[524,128]{1,0:T(8,128)S(1)} %pad_maximum_fusion), channel_id=1, source_target_pairs={{4,0},{5,1},{6,2},{7,3},{8,4},{9,5},{10,6},{11,7},{12,8},{13,9},{1... | collective-permute-start | bytes 804872 | tf_op jit(solution)/shard_map/ppermute | solution.py:24
  397.9 39.6 %collective-permute-start.12 = (f32[524,128]{1,0:T(8,128)S(1)}, f32[524,128]{1,0:T(8,128)S(1)}, u32[]{:S(2)}, u32[]{:S(2)}) collective-permute-start(f32[524,128]{1,0:T(8,128)S(1)} %pad_maximum_fusion), channel_id=1, source_target_pairs={{5,0},{6,1},{7,2},{8,3},{9,4},{10,5},{11,6},{12,7},{13,8},{14,9},{... | collective-permute-start | bytes 804872 | tf_op jit(solution)/shard_map/ppermute | solution.py:24
  401.3 48.8 %collective-permute-start.13 = (f32[524,128]{1,0:T(8,128)S(1)}, f32[524,128]{1,0:T(8,128)S(1)}, u32[]{:S(2)}, u32[]{:S(2)}) collective-permute-start(f32[524,128]{1,0:T(8,128)S(1)} %pad_maximum_fusion), channel_id=1, source_target_pairs={{6,0},{7,1},{8,2},{9,3},{10,4},{11,5},{12,6},{13,7},{14,8},{15,9},... | collective-permute-start | bytes 804872 | tf_op jit(solution)/shard_map/ppermute | solution.py:24
  404.4 199.2 %collective-permute-start.14 = (f32[524,128]{1,0:T(8,128)S(1)}, f32[524,128]{1,0:T(8,128)S(1)}, u32[]{:S(2)}, u32[]{:S(2)}) collective-permute-start(f32[524,128]{1,0:T(8,128)S(1)} %pad_maximum_fusion), channel_id=1, source_target_pairs={{7,0},{8,1},{9,2},{10,3},{11,4},{12,5},{13,6},{14,7},{15,8},{16,9}... | collective-permute-start | bytes 804872 | tf_op jit(solution)/shard_map/ppermute | solution.py:24
  410.5 197.4 %collective-permute-start.15 = (f32[524,128]{1,0:T(8,128)S(1)}, f32[524,128]{1,0:T(8,128)S(1)}, u32[]{:S(2)}, u32[]{:S(2)}) collective-permute-start(f32[524,128]{1,0:T(8,128)S(1)} %pad_maximum_fusion), channel_id=1, source_target_pairs={{8,0},{9,1},{10,2},{11,3},{12,4},{13,5},{14,6},{15,7},{16,8},{17,9... | collective-permute-start | bytes 804872 | tf_op jit(solution)/shard_map/ppermute | solution.py:24
  601.4 3.1 collective-permute-start.54
  604.5 5.8 collective-permute-start.55
  610.5 83.1 %collective-permute-start.56 = (f32[64,128]{1,0:T(8,128)S(1)}, f32[64,128]{1,0:T(8,128)S(1)}, u32[]{:S(2)}, u32[]{:S(2)}) collective-permute-start(f32[64,128]{1,0:T(8,128)S(1)} %add.202), channel_id=1, source_target_pairs={{0,1},{1,0},{2,3},{3,2},{4,5},{5,4},{6,7},{7,6},{8,9},{9,8},{10,11... | collective-permute-start | bytes 98312 | tf_op jit(solution)/shard_map/ppermute | solution.py:18
  612.5 81.2 %copy-start.2 = (f32[1,128,128]{2,1,0:T(8,128)S(1)}, f32[1,128,128]{2,1,0:T(8,128)}, u32[]{:S(2)}) copy-start(f32[1,128,128]{2,1,0:T(8,128)} %param.28) | copy-start | bytes 196612
  (2 other events, 2.0 us)
Sparse Core Ops, SparseCore 0:
  311.3 259.5 all-gather.1
where the time goes:
time: 710 us; the launch traced here: 702 us
  starting transfers between devices  248 us (35%)
  waiting for transfers between devices  223 us (31%)
  local copies, waits for them, and re-layouts  85.7 us (12%)
  matrix products  64.8 us (9%)
  loops' own time  63 us (9%)
  between operations  14.8 us (2%)
    ppermute x48, starting transfers between devices, from_behind(): return lax.ppermute(block, axis, route)  226 us
    all_gather x1, waiting for transfers between devices, per_device(): lax.all_gather(top_rows_own, 'leaf', axis=0, tiled=True)  120 us
    ppermute x48, waiting for transfers between devices, from_behind(): return lax.ppermute(block, axis, route)  85.8 us
    another operation x5, loops' own time, listed_sum(): result, _ = lax.scan(advance, start_value, entries)  63 us
    dot_general x48, matrix products, advance(): jnp.dot(kernel_block(own_coords, coords), values, precision=HIGHEST)  59.8 us
    sub x80, local copies, waits for them, and re-layouts, kernel_block(): offset_gap = left_pts[axis_id][:, None] - right_pts[axis_id][None, :]  36.5 us
    dynamic_slice x48, local copies, waits for them, and re-layouts, listed_sum(): result, _ = lax.scan(advance, start_value, entries)  28.5 us
    ppermute x9, starting transfers between devices, from_partner(): return lax.ppermute(value, axis, pairs)  21.2 us
  transfers between devices with their start and end apart: 58, of which 19 were waited for; matrix products, arithmetic and copies ran while one was open for 21% of the time, Pallas kernels for 0%

commit v1 on v0

v1 whole, which is shorter than its diff:
```python
import jax
import jax.numpy as jnp
from jax import lax
from jax.sharding import Mesh
from jax.sharding import PartitionSpec as P

REACH = 8
FAR_REACH = 4


INV_FOUR_PI = 0.07957747154594767
DELTA_SQ = 0.01
HIGHEST = lax.Precision.HIGHEST

AX = ("cl", "q", "p", "c")
MEMBERS = ("q", "p", "c")


def from_partner(value, axis, bit):
    mask = 2**bit
    pairs = [(source, source ^ mask) for source in range(lax.axis_size(axis))]
    return lax.ppermute(value, axis, pairs)


def from_behind(block, axis, distance):
    devices = range(lax.axis_size(axis))
    route = [(i - distance, i) for i in devices if i - distance in devices]
    return lax.ppermute(block, axis, route)


def kernel_block(left_pts, right_pts):
    distance = jnp.zeros((left_pts.shape[1], right_pts.shape[1]), jnp.float32)
    for axis_id in range(3):
        offset_gap = left_pts[axis_id][:, None] - right_pts[axis_id][None, :]
        distance = distance + offset_gap * offset_gap
    return INV_FOUR_PI * lax.rsqrt(distance + DELTA_SQ)


def transposed_dot(matrix, values):
    return lax.dot_general(matrix, values, (((0,), (0,)), ((), ())), precision=HIGHEST)


def listed_sum(own_coords, entries, fetcher, width):

    def advance(running, partner):
        coords, values = fetcher(jnp.maximum(partner, 0))
        contrib = jnp.dot(kernel_block(own_coords, coords), values, precision=HIGHEST)
        return (running + jnp.where(partner >= 0, contrib, 0.0), None)

    start_value = jnp.zeros((own_coords.shape[1], width), jnp.float32)
    result, _ = lax.scan(advance, start_value, entries)
    return result


def batched_far(own_coords, coords, values, valid):
    count, _, span = coords.shape
    right = jnp.transpose(coords, (1, 0, 2)).reshape(3, count * span)
    masked = jnp.where(valid[:, None, None], values, 0.0)
    flat = masked.reshape(count * span, values.shape[2])
    return jnp.dot(kernel_block(own_coords, right), flat, precision=HIGHEST)


def pair_total(partial_value, levels):
    for bit_index in range(levels):
        partial_value = partial_value + from_partner(partial_value, AX, bit_index)
    return partial_value


def join_rows(block, levels, device):
    for bit_index in range(levels):
        other = from_partner(block, AX, bit_index)
        upper = device // 2**bit_index % 2
        block = jnp.where(
            upper == 0, jnp.concatenate([block, other], 0), jnp.concatenate([other, block], 0)
        )
    return block


def window(shipped):
    gathered = []
    for distance in range(-REACH, REACH + 1):
        if distance == 0:
            gathered.append(shipped)
        else:
            gathered.append(from_behind(shipped, AX, -distance))
    return jnp.stack(gathered)


def partner_stack(coefs, stride):
    gathered = []
    for offset in list(range(-FAR_REACH, 0)) + list(range(1, FAR_REACH + 1)):
        gathered.append(from_behind(coefs, AX, -offset * stride))
    stacked = jnp.stack(gathered)

    def slot_of(distance):
        return distance + FAR_REACH - (distance > 0).astype(jnp.int32)

    return (stacked, slot_of)


def middle_level(coefs, skeletons, lists, transfer_rows, above, stride, device):
    rank_rows = coefs.shape[0] // stride
    cluster = device // stride
    member = device % stride
    own_full = lax.dynamic_index_in_dim(skeletons, cluster, 0, keepdims=False)
    own_coords = lax.dynamic_slice_in_dim(own_full, member * rank_rows, rank_rows, 1)
    stacked, slot_of = partner_stack(coefs, stride)
    entries = lax.dynamic_index_in_dim(lists, cluster, 0, keepdims=False)
    chosen = jnp.maximum(entries, 0)
    coords = jnp.take(skeletons, chosen, axis=0)
    slots = jnp.clip(slot_of(chosen - cluster), 0, stacked.shape[0] - 1)
    values = jnp.take(stacked, slots, axis=0)
    rows_here = batched_far(own_coords, coords, values, entries >= 0) + jnp.dot(
        transfer_rows, above, precision=HIGHEST
    )
    return join_rows(rows_here, stride.bit_length() - 1, device)


def per_device(
    vectors,
    points,
    leaf_basis,
    transfer_leaf,
    transfer_pair,
    transfer_quad,
    skel_leaf,
    skel_pair,
    skel_quad,
    skel_top,
    near_list,
    far_leaf,
    far_pair,
    far_quad,
    far_top,
):
    leaf_points = vectors.shape[1]
    width = vectors.shape[2]
    rank = leaf_basis.shape[2]
    device = lax.axis_index(AX)
    own_points = points[0]
    shipped = jnp.concatenate(
        [vectors[0], own_points.reshape(3 * leaf_points // width, width)], axis=0
    )
    near_rim = window(shipped)

    def near_fetch(partner):
        position = jnp.clip(partner - device + REACH, 0, 2 * REACH)
        block = lax.dynamic_index_in_dim(near_rim, position, 0, keepdims=False)
        return (block[leaf_points:].reshape(3, leaf_points), block[:leaf_points])

    near_field = listed_sum(own_points, near_list[0], near_fetch, width)
    coef_leaf = transposed_dot(leaf_basis[0], vectors[0])
    coef_pair = pair_total(transposed_dot(transfer_leaf[0], coef_leaf), 1)
    pair_rows = lax.dynamic_slice_in_dim(coef_pair, device % 2 * (rank // 2), rank // 2, 0)
    coef_quad = pair_total(transposed_dot(transfer_pair, pair_rows), 2)
    quad_rows = lax.dynamic_slice_in_dim(coef_quad, device % 4 * (rank // 4), rank // 4, 0)
    coef_top = pair_total(transposed_dot(transfer_quad, quad_rows), 3)
    top_cluster = device // 8
    top_member = device % 8
    share = width // 8
    top_cols_own = lax.dynamic_slice_in_dim(coef_top, top_member * share, share, 1)
    all_top = lax.all_gather(top_cols_own, "cl", axis=0)
    top_coords = lax.dynamic_index_in_dim(skel_top, top_cluster, 0, keepdims=False)
    top_entries = lax.dynamic_index_in_dim(far_top, top_cluster, 0, keepdims=False)
    top_chosen = jnp.maximum(top_entries, 0)
    top_cols = batched_far(
        top_coords,
        jnp.take(skel_top, top_chosen, axis=0),
        jnp.take(all_top, top_chosen, axis=0),
        top_entries >= 0,
    )
    local_top = lax.all_gather(top_cols, MEMBERS, axis=1, tiled=True)
    local_quad = middle_level(coef_quad, skel_quad, far_quad, transfer_quad, local_top, 4, device)
    local_pair = middle_level(coef_pair, skel_pair, far_pair, transfer_pair, local_quad, 2, device)
    leaf_ship = jnp.concatenate([coef_leaf, skel_leaf[0]], axis=0)
    leaf_rim = window(leaf_ship)
    leaf_entries = far_leaf[0]
    positions = jnp.clip(jnp.maximum(leaf_entries, 0) - device + REACH, 0, 2 * REACH)
    leaf_blocks = jnp.take(leaf_rim, positions, axis=0)
    local_leaf = batched_far(
        skel_leaf[0], leaf_blocks[:, rank:], leaf_blocks[:, :rank], leaf_entries >= 0
    ) + jnp.dot(transfer_leaf[0], local_pair, precision=HIGHEST)
    product = near_field + jnp.dot(leaf_basis[0], local_leaf, precision=HIGHEST)
    return product[None]


def solution(mesh):
    count = mesh.devices.size
    grid = Mesh(mesh.devices.reshape(count // 8, 2, 2, 2), AX)
    spread = P(AX, None, None)
    rows = P(AX, None)
    placed = (
        spread,
        spread,
        spread,
        spread,
        rows,
        rows,
        spread,
        P(),
        P(),
        P(),
        rows,
        rows,
        P(),
        P(),
        P(),
    )
    return jax.shard_map(per_device, mesh=grid, in_specs=placed, out_specs=spread, check_vma=False)
```

time: 710 us -> 804 us (1.13)
  blocking collectives: 0 us -> 214 us
  loops' own time: 63 us -> 18.3 us
  starting transfers between devices: 248 us -> 210 us
  local copies, waits for them, and re-layouts: 85.7 us -> 53.3 us
  matrix products: 64.8 us -> 47.3 us
  between operations: 14.8 us -> 1.55 us
  waiting for transfers between devices: 223 us -> 236 us
    all_gather x0 -> x2, blocking collectives: none -> 214 us  [the longest x1 200 us: per_device(): all_top = lax.all_gather(top_cols_own, 'cl', axis=0)]
    all_gather x1 -> x0, waiting for transfers between devices: 120 us -> none  [per_device(): lax.all_gather(top_rows_own, 'leaf', axis=0, tiled=True)]
    ppermute x48, waiting for transfers between devices: 85.8 us -> 162 us  [from_behind(): return lax.ppermute(block, axis, route)]
    ppermute x9, waiting for transfers between devices: 17.3 us -> 73.6 us  [from_partner(): return lax.ppermute(value, axis, pairs)]
    another operation x5 -> x1, loops' own time: 63 us -> 18.3 us  [listed_sum(): result, _ = lax.scan(advance, start_value, entries)]
    ppermute x48, starting transfers between devices: 226 us -> 192 us  [from_behind(): return lax.ppermute(block, axis, route)]
    dot_general x48 -> x16, matrix products: 59.8 us -> 37.6 us  [advance(): jnp.dot(kernel_block(own_coords, coords), values, precision=HIGHEST)]
    dynamic_slice x48 -> x16, local copies, waits for them, and re-layouts: 28.5 us -> 8.85 us  [listed_sum(): result, _ = lax.scan(advance, start_value, entries)]
  transfers between devices with their start and end apart: 58 -> 57, of which waited for: 19 -> 21; matrix products, arithmetic and copies ran while one was open for 21% -> 14% of each run, Pallas kernels for 0% -> 0%
where the time goes in v1:
time: 804 us; the launch traced here: 791 us
  waiting for transfers between devices  236 us (29%)
  blocking collectives  214 us (27%)
  starting transfers between devices  210 us (26%)
  local copies, waits for them, and re-layouts  53.3 us (7%)
  matrix products  47.3 us (6%)
  loops' own time  18.3 us (2%)
  other arithmetic  10.6 us (1%)
    all_gather x1, blocking collectives, per_device(): all_top = lax.all_gather(top_cols_own, 'cl', axis=0)  200 us
    ppermute x48, starting transfers between devices, from_behind(): return lax.ppermute(block, axis, route)  192 us
    ppermute x48, waiting for transfers between devices, from_behind(): return lax.ppermute(block, axis, route)  162 us
    ppermute x9, waiting for transfers between devices, from_partner(): return lax.ppermute(value, axis, pairs)  73.6 us
    dot_general x16, matrix products, advance(): jnp.dot(kernel_block(own_coords, coords), values, precision=HIGHEST)  37.6 us
    sub x23, local copies, waits for them, and re-layouts, kernel_block(): offset_gap = left_pts[axis_id][:, None] - right_pts[axis_id][None, :]  18.9 us
    another operation x1, loops' own time, listed_sum(): result, _ = lax.scan(advance, start_value, entries)  18.3 us
    ppermute x9, starting transfers between devices, from_partner(): return lax.ppermute(value, axis, pairs)  17.6 us
  transfers between devices with their start and end apart: 57, of which 21 were waited for; matrix products, arithmetic and copies ran while one was open for 14% of the time, Pallas kernels for 0%

profile of v1, /device:TPU:24, one launch (start us, length us, event | category | flops | bytes accessed | tf_op | source)
XLA Modules:
  0.0 791.2 jit_solution(14882658915366120333)
XLA Ops:
  2.5 9.1 %collective-permute-start.16 = (f32[131,128]{1,0:T(8,128)S(1)}, f32[131,128]{1,0:T(8,128)S(1)}, u32[]{:S(2)}, u32[]{:S(2)}) collective-permute-start(f32[131,128]{1,0:T(8,128)S(1)} %pad_maximum_fusion.1), channel_id=1, source_target_pairs={{0,8},{1,9},{2,10},{3,11},{4,12},{5,13},{6,14},{7,15},{8,16},{9,17... | collective-permute-start | bytes 201224 | tf_op jit(solution)/shard_map/ppermute | solution.py:28
  11.6 5.7 collective-permute-start.17
  17.3 5.9 collective-permute-start.18
  23.3 4.1 collective-permute-start.19
  53.7 3.4 collective-permute-start.20
  60.2 2.6 collective-permute-start.22
  65.1 7.5 collective-permute-start.24
  72.6 3.3 collective-permute-start.25
  75.9 2.9 collective-permute-start.26
  78.9 4.6 collective-permute-start.27
  83.5 4.1 collective-permute-start.28
  87.6 4.0 collective-permute-start.29
  93.9 5.7 collective-permute-start.31
  99.7 4.0 collective-permute-start
  103.7 4.6 collective-permute-start.1
  108.4 4.8 collective-permute-start.2
  113.2 4.3 collective-permute-start.33
  117.5 4.8 collective-permute-start.34
  125.4 53.5 %collective-permute-done.33 = f32[128,128]{1,0:T(8,128)} collective-permute-done((f32[128,128]{1,0:T(8,128)S(1)}, f32[128,128]{1,0:T(8,128)}, u32[]{:S(2)}, u32[]{:S(2)}) %collective-permute-start.33) | collective-permute-done | bytes 65568 | tf_op jit(solution)/shard_map/ppermute | solution.py:28
  181.7 2.6 collective-permute-start.36
  185.2 5.0 collective-permute-done.35
  190.2 2.4 collective-permute-start.37
  192.6 4.8 collective-permute-start.38
  197.5 4.0 collective-permute-start.39
  201.5 3.9 collective-permute-start.40
  210.2 7.6 collective-permute-start.3
  221.8 10.1 %collective-permute-done.42 = f32[128,128]{1,0:T(8,128)S(1)} collective-permute-done((f32[128,128]{1,0:T(8,128)S(1)}, f32[128,128]{1,0:T(8,128)S(1)}, u32[]{:S(2)}, u32[]{:S(2)}) %collective-permute-start.42) | collective-permute-done | bytes 65568 | tf_op jit(solution)/shard_map/ppermute | solution.py:22
  234.2 17.5 %collective-permute-done.43 = f32[128,128]{1,0:T(8,128)S(1)} collective-permute-done((f32[128,128]{1,0:T(8,128)S(1)}, f32[128,128]{1,0:T(8,128)S(1)}, u32[]{:S(2)}, u32[]{:S(2)}) %collective-permute-start.43) | collective-permute-done | bytes 65568 | tf_op jit(solution)/shard_map/ppermute | solution.py:28
  253.6 14.1 %collective-permute-done.44 = f32[128,128]{1,0:T(8,128)S(1)} collective-permute-done((f32[128,128]{1,0:T(8,128)S(1)}, f32[128,128]{1,0:T(8,128)S(1)}, u32[]{:S(2)}, u32[]{:S(2)}) %collective-permute-start.44) | collective-permute-done | bytes 65568 | tf_op jit(solution)/shard_map/ppermute | solution.py:28
  269.7 11.2 %collective-permute-done.45 = f32[128,128]{1,0:T(8,128)S(1)} collective-permute-done((f32[128,128]{1,0:T(8,128)S(1)}, f32[128,128]{1,0:T(8,128)S(1)}, u32[]{:S(2)}, u32[]{:S(2)}) %collective-permute-start.45) | collective-permute-done | bytes 65568 | tf_op jit(solution)/shard_map/ppermute | solution.py:28
  282.8 9.3 %collective-permute-done.46 = f32[128,128]{1,0:T(8,128)S(1)} collective-permute-done((f32[128,128]{1,0:T(8,128)S(1)}, f32[128,128]{1,0:T(8,128)S(1)}, u32[]{:S(2)}, u32[]{:S(2)}) %collective-permute-start.46) | collective-permute-done | bytes 65568 | tf_op jit(solution)/shard_map/ppermute | solution.py:28
  294.0 5.1 collective-permute-done.47
  301.1 8.1 %collective-permute-done.48 = f32[128,128]{1,0:T(8,128)S(1)} collective-permute-done((f32[128,128]{1,0:T(8,128)S(1)}, f32[128,128]{1,0:T(8,128)S(1)}, u32[]{:S(2)}, u32[]{:S(2)}) %collective-permute-start.48) | collective-permute-done | bytes 65568 | tf_op jit(solution)/shard_map/ppermute | solution.py:28
  309.2 5.8 collective-permute-start.49
  315.0 6.0 collective-permute-done.49
  321.1 8.6 %collective-permute-start.50 = (f32[128,128]{1,0:T(8,128)S(1)}, f32[128,128]{1,0:T(8,128)S(1)}, u32[]{:S(2)}, u32[]{:S(2)}) collective-permute-start(f32[128,128]{1,0:T(8,128)S(1)} %add.237), channel_id=1, source_target_pairs={{16,0},{17,1},{18,2},{19,3},{20,4},{21,5},{22,6},{23,7},{24,8},{25... | collective-permute-start | bytes 196616 | tf_op jit(solution)/shard_map/ppermute | solution.py:28
  329.7 7.5 collective-permute-done.50
  340.6 3.3 collective-permute-start.4
  343.9 4.7 collective-permute-start.5
  349.4 2.4 collective-permute-start.6
  352.5 4.5 collective-permute-start.7
  357.8 10.1 %collective-permute-start.8 = (f32[524,128]{1,0:T(8,128)S(1)}, f32[524,128]{1,0:T(8,128)S(1)}, u32[]{:S(2)}, u32[]{:S(2)}) collective-permute-start(f32[524,128]{1,0:T(8,128)S(1)} %pad_maximum_fusion), channel_id=1, source_target_pairs={{1,0},{2,1},{3,2},{4,3},{5,4},{6,5},{7,6},{8,7},{9,8},{10,9},{11,1... | collective-permute-start | bytes 804872 | tf_op jit(solution)/shard_map/ppermute | solution.py:28
  369.2 3.1 collective-permute-start.9
  373.0 3.3 collective-permute-done.5
  376.3 6.3 collective-permute-start.10
  383.4 5.3 collective-permute-start.11
  400.9 11.1 %collective-permute-done.11 = f32[524,128]{1,0:T(8,128)S(1)} collective-permute-done((f32[524,128]{1,0:T(8,128)S(1)}, f32[524,128]{1,0:T(8,128)S(1)}, u32[]{:S(2)}, u32[]{:S(2)}) %collective-permute-start.11) | collective-permute-done | bytes 268320 | tf_op jit(solution)/shard_map/ppermute | solution.py:28
  414.6 8.3 %collective-permute-done.12 = f32[524,128]{1,0:T(8,128)S(1)} collective-permute-done((f32[524,128]{1,0:T(8,128)S(1)}, f32[524,128]{1,0:T(8,128)S(1)}, u32[]{:S(2)}, u32[]{:S(2)}) %collective-permute-start.12) | collective-permute-done | bytes 268320 | tf_op jit(solution)/shard_map/ppermute | solution.py:28
  423.7 54.6 %collective-permute-done.52 = f32[128,128]{0,1:T(8,128)S(1)} collective-permute-done((f32[128,128]{0,1:T(8,128)S(1)}, f32[128,128]{0,1:T(8,128)S(1)}, u32[]{:S(2)}, u32[]{:S(2)}) %collective-permute-start.52) | collective-permute-done | bytes 65568 | tf_op jit(solution)/shard_map/ppermute | solution.py:22
  481.0 4.4 collective-permute-done.53
  485.4 200.0 %all-gather = f32[8192,16]{0,1:T(8,128)S(1)} all-gather(f32[128,16]{0,1:T(8,128)S(1)} %dynamic-slice_add_fusion), channel_id=2, replica_groups=mesh['cl'=64,'q'=2,'p'=2,'c'=2] {'cl'}, dimensions={0}, use_global_device_ids=true | all-gather | bytes 532480 | tf_op jit(solution)/shard_map/all_gather | solution.py:162
  687.0 14.0 %all_gather.11 = f32[128,128]{0,1:T(8,128)S(1)} all-gather(f32[128,16]{0,1:T(8,128)S(1)} %fusion.28), channel_id=1, replica_groups=mesh['cl'=64,'q'=2,'p'=2,'c'=2] {'q','p','c'}, dimensions={1}, use_global_device_ids=true | all-gather | bytes 73728 | tf_op jit(solution)/shard_map/all_gather | solution.py:172
  707.0 3.1 collective-permute-done.55
  712.3 77.2 %while.11 = (s32[]{:T(128)}, f32[512,128]{1,0:T(8,128)S(1)}, s32[16]{0:T(128)S(1)}, f32[3,512]{1,0:T(4,128)S(1)}, s32[]{:T(128)}, /*index=5*/f32[17,524,128]{2,1...) while((s32[]{:T(128)}, f32[512,128]{1,0:T(8,128)S(1)}, ...), condition=%wide.region_1.2_spmd.clone, body=%wide.region_0.1_spmd.clone.sunk | while | flops 405471232 | bytes 824088 | solution.py:51
  714.7 2.4 fusion.174
  719.6 2.4 fusion.174
  724.4 2.4 fusion.174
  729.2 2.4 fusion.174
  734.0 2.4 fusion.174
  738.9 2.4 fusion.174
  743.7 2.4 fusion.174
  748.5 2.4 fusion.174
  758.2 2.4 fusion.174
  767.8 2.4 fusion.174
  (288 shorter events, 136.5 us)
Async XLA Ops:
  2.5 55.7 %collective-permute-start.16 = (f32[131,128]{1,0:T(8,128)S(1)}, f32[131,128]{1,0:T(8,128)S(1)}, u32[]{:S(2)}, u32[]{:S(2)}) collective-permute-start(f32[131,128]{1,0:T(8,128)S(1)} %pad_maximum_fusion.1), channel_id=1, source_target_pairs={{0,8},{1,9},{2,10},{3,11},{4,12},{5,13},{6,14},{7,15},{8,16},{9,17... | collective-permute-start | bytes 201224 | tf_op jit(solution)/shard_map/ppermute | solution.py:28
  11.6 48.5 %collective-permute-start.17 = (f32[131,128]{1,0:T(8,128)S(1)}, f32[131,128]{1,0:T(8,128)S(1)}, u32[]{:S(2)}, u32[]{:S(2)}) collective-permute-start(f32[131,128]{1,0:T(8,128)S(1)} %pad_maximum_fusion.1), channel_id=1, source_target_pairs={{0,7},{1,8},{2,9},{3,10},{4,11},{5,12},{6,13},{7,14},{8,15},{9,16}... | collective-permute-start | bytes 201224 | tf_op jit(solution)/shard_map/ppermute | solution.py:28
  17.3 45.4 %collective-permute-start.18 = (f32[131,128]{1,0:T(8,128)S(1)}, f32[131,128]{1,0:T(8,128)S(1)}, u32[]{:S(2)}, u32[]{:S(2)}) collective-permute-start(f32[131,128]{1,0:T(8,128)S(1)} %pad_maximum_fusion.1), channel_id=1, source_target_pairs={{0,6},{1,7},{2,8},{3,9},{4,10},{5,11},{6,12},{7,13},{8,14},{9,15},... | collective-permute-start | bytes 201224 | tf_op jit(solution)/shard_map/ppermute | solution.py:28
  23.3 41.8 %collective-permute-start.19 = (f32[131,128]{1,0:T(8,128)S(1)}, f32[131,128]{1,0:T(8,128)S(1)}, u32[]{:S(2)}, u32[]{:S(2)}) collective-permute-start(f32[131,128]{1,0:T(8,128)S(1)} %pad_maximum_fusion.1), channel_id=1, source_target_pairs={{0,5},{1,6},{2,7},{3,8},{4,9},{5,10},{6,11},{7,12},{8,13},{9,14},{... | collective-permute-start | bytes 201224 | tf_op jit(solution)/shard_map/ppermute | solution.py:28
  28.5 25.2 %collective-permute-start.32 = (f32[128,128]{1,0:T(8,128)S(1)}, f32[128,128]{1,0:T(8,128)S(1)}, u32[]{:S(2)}, u32[]{:S(2)}) collective-permute-start(f32[128,128]{1,0:T(8,128)S(1)} %convolution_bitcast_fusion.4), channel_id=1, source_target_pairs={{0,1},{1,0},{2,3},{3,2},{4,5},{5,4},{6,7},{7,6},{8,9},{9,8},{10,11... | collective-permute-start | bytes 196616 | tf_op jit(solution)/shard_map/ppermute | solution.py:22
  53.7 18.9 %collective-permute-start.20 = (f32[131,128]{1,0:T(8,128)S(1)}, f32[131,128]{1,0:T(8,128)S(1)}, u32[]{:S(2)}, u32[]{:S(2)}) collective-permute-start(f32[131,128]{1,0:T(8,128)S(1)} %pad_maximum_fusion.1), channel_id=1, source_target_pairs={{0,4},{1,5},{2,6},{3,7},{4,8},{5,9},{6,10},{7,11},{8,12},{9,13},{1... | collective-permute-start | bytes 201224 | tf_op jit(solution)/shard_map/ppermute | solution.py:28
  58.2 17.7 %collective-permute-start.21 = (f32[131,128]{1,0:T(8,128)S(1)}, f32[131,128]{1,0:T(8,128)S(1)}, u32[]{:S(2)}, u32[]{:S(2)}) collective-permute-start(f32[131,128]{1,0:T(8,128)S(1)} %pad_maximum_fusion.1), channel_id=1, source_target_pairs={{0,3},{1,4},{2,5},{3,6},{4,7},{5,8},{6,9},{7,10},{8,11},{9,12},{10... | collective-permute-start | bytes 201224 | tf_op jit(solution)/shard_map/ppermute | solution.py:28
  60.2 18.7 %collective-permute-start.22 = (f32[131,128]{1,0:T(8,128)S(1)}, f32[131,128]{1,0:T(8,128)S(1)}, u32[]{:S(2)}, u32[]{:S(2)}) collective-permute-start(f32[131,128]{1,0:T(8,128)S(1)} %pad_maximum_fusion.1), channel_id=1, source_target_pairs={{0,2},{1,3},{2,4},{3,5},{4,6},{5,7},{6,8},{7,9},{8,10},{9,11},{10,... | collective-permute-start | bytes 201224 | tf_op jit(solution)/shard_map/ppermute | solution.py:28
  62.8 20.7 %collective-permute-start.23 = (f32[131,128]{1,0:T(8,128)S(1)}, f32[131,128]{1,0:T(8,128)S(1)}, u32[]{:S(2)}, u32[]{:S(2)}) collective-permute-start(f32[131,128]{1,0:T(8,128)S(1)} %pad_maximum_fusion.1), channel_id=1, source_target_pairs={{0,1},{1,2},{2,3},{3,4},{4,5},{5,6},{6,7},{7,8},{8,9},{9,10},{10,1... | collective-permute-start | bytes 201224 | tf_op jit(solution)/shard_map/ppermute | solution.py:28
  65.1 22.5 %collective-permute-start.24 = (f32[131,128]{1,0:T(8,128)S(1)}, f32[131,128]{1,0:T(8,128)S(1)}, u32[]{:S(2)}, u32[]{:S(2)}) collective-permute-start(f32[131,128]{1,0:T(8,128)S(1)} %pad_maximum_fusion.1), channel_id=1, source_target_pairs={{1,0},{2,1},{3,2},{4,3},{5,4},{6,5},{7,6},{8,7},{9,8},{10,9},{11,1... | collective-permute-start | bytes 201224 | tf_op jit(solution)/shard_map/ppermute | solution.py:28
  72.6 19.0 %collective-permute-start.25 = (f32[131,128]{1,0:T(8,128)S(1)}, f32[131,128]{1,0:T(8,128)S(1)}, u32[]{:S(2)}, u32[]{:S(2)}) collective-permute-start(f32[131,128]{1,0:T(8,128)S(1)} %pad_maximum_fusion.1), channel_id=1, source_target_pairs={{2,0},{3,1},{4,2},{5,3},{6,4},{7,5},{8,6},{9,7},{10,8},{11,9},{12,... | collective-permute-start | bytes 201224 | tf_op jit(solution)/shard_map/ppermute | solution.py:28
  75.9 18.0 %collective-permute-start.26 = (f32[131,128]{1,0:T(8,128)S(1)}, f32[131,128]{1,0:T(8,128)S(1)}, u32[]{:S(2)}, u32[]{:S(2)}) collective-permute-start(f32[131,128]{1,0:T(8,128)S(1)} %pad_maximum_fusion.1), channel_id=1, source_target_pairs={{3,0},{4,1},{5,2},{6,3},{7,4},{8,5},{9,6},{10,7},{11,8},{12,9},{13... | collective-permute-start | bytes 201224 | tf_op jit(solution)/shard_map/ppermute | solution.py:28
  78.9 20.8 %collective-permute-start.27 = (f32[131,128]{1,0:T(8,128)S(1)}, f32[131,128]{1,0:T(8,128)S(1)}, u32[]{:S(2)}, u32[]{:S(2)}) collective-permute-start(f32[131,128]{1,0:T(8,128)S(1)} %pad_maximum_fusion.1), channel_id=1, source_target_pairs={{4,0},{5,1},{6,2},{7,3},{8,4},{9,5},{10,6},{11,7},{12,8},{13,9},{1... | collective-permute-start | bytes 201224 | tf_op jit(solution)/shard_map/ppermute | solution.py:28
  83.5 20.2 %collective-permute-start.28 = (f32[131,128]{1,0:T(8,128)S(1)}, f32[131,128]{1,0:T(8,128)S(1)}, u32[]{:S(2)}, u32[]{:S(2)}) collective-permute-start(f32[131,128]{1,0:T(8,128)S(1)} %pad_maximum_fusion.1), channel_id=1, source_target_pairs={{5,0},{6,1},{7,2},{8,3},{9,4},{10,5},{11,6},{12,7},{13,8},{14,9},{... | collective-permute-start | bytes 201224 | tf_op jit(solution)/shard_map/ppermute | solution.py:28
  87.6 20.7 %collective-permute-start.29 = (f32[131,128]{1,0:T(8,128)S(1)}, f32[131,128]{1,0:T(8,128)S(1)}, u32[]{:S(2)}, u32[]{:S(2)}) collective-permute-start(f32[131,128]{1,0:T(8,128)S(1)} %pad_maximum_fusion.1), channel_id=1, source_target_pairs={{6,0},{7,1},{8,2},{9,3},{10,4},{11,5},{12,6},{13,7},{14,8},{15,9},... | collective-permute-start | bytes 201224 | tf_op jit(solution)/shard_map/ppermute | solution.py:28
  91.7 21.5 %collective-permute-start.30 = (f32[131,128]{1,0:T(8,128)S(1)}, f32[131,128]{1,0:T(8,128)S(1)}, u32[]{:S(2)}, u32[]{:S(2)}) collective-permute-start(f32[131,128]{1,0:T(8,128)S(1)} %pad_maximum_fusion.1), channel_id=1, source_target_pairs={{7,0},{8,1},{9,2},{10,3},{11,4},{12,5},{13,6},{14,7},{15,8},{16,9}... | collective-permute-start | bytes 201224 | tf_op jit(solution)/shard_map/ppermute | solution.py:28
  93.9 23.6 %collective-permute-start.31 = (f32[131,128]{1,0:T(8,128)S(1)}, f32[131,128]{1,0:T(8,128)S(1)}, u32[]{:S(2)}, u32[]{:S(2)}) collective-permute-start(f32[131,128]{1,0:T(8,128)S(1)} %pad_maximum_fusion.1), channel_id=1, source_target_pairs={{8,0},{9,1},{10,2},{11,3},{12,4},{13,5},{14,6},{15,7},{16,8},{17,9... | collective-permute-start | bytes 201224 | tf_op jit(solution)/shard_map/ppermute | solution.py:28
  99.7 244.3 %collective-permute-start = (f32[524,128]{1,0:T(8,128)S(1)}, f32[524,128]{1,0:T(8,128)S(1)}, u32[]{:S(2)}, u32[]{:S(2)}) collective-permute-start(f32[524,128]{1,0:T(8,128)S(1)} %pad_maximum_fusion), channel_id=1, source_target_pairs={{0,8},{1,9},{2,10},{3,11},{4,12},{5,13},{6,14},{7,15},{8,16},{9,17... | collective-permute-start | bytes 804872 | tf_op jit(solution)/shard_map/ppermute | solution.py:28
  103.7 245.6 %collective-permute-start.1 = (f32[524,128]{1,0:T(8,128)S(1)}, f32[524,128]{1,0:T(8,128)S(1)}, u32[]{:S(2)}, u32[]{:S(2)}) collective-permute-start(f32[524,128]{1,0:T(8,128)S(1)} %pad_maximum_fusion), channel_id=1, source_target_pairs={{0,7},{1,8},{2,9},{3,10},{4,11},{5,12},{6,13},{7,14},{8,15},{9,16}... | collective-permute-start | bytes 804872 | tf_op jit(solution)/shard_map/ppermute | solution.py:28
  108.4 244.2 %collective-permute-start.2 = (f32[524,128]{1,0:T(8,128)S(1)}, f32[524,128]{1,0:T(8,128)S(1)}, u32[]{:S(2)}, u32[]{:S(2)}) collective-permute-start(f32[524,128]{1,0:T(8,128)S(1)} %pad_maximum_fusion), channel_id=1, source_target_pairs={{0,6},{1,7},{2,8},{3,9},{4,10},{5,11},{6,12},{7,13},{8,14},{9,15},... | collective-permute-start | bytes 804872 | tf_op jit(solution)/shard_map/ppermute | solution.py:28
  113.2 65.7 %collective-permute-start.33 = (f32[128,128]{1,0:T(8,128)S(1)}, f32[128,128]{1,0:T(8,128)}, u32[]{:S(2)}, u32[]{:S(2)}) collective-permute-start(f32[128,128]{1,0:T(8,128)S(1)} %add.225), channel_id=1, source_target_pairs={{0,8},{1,9},{2,10},{3,11},{4,12},{5,13},{6,14},{7,15},{8,16},{9,17... | collective-permute-start | bytes 196616 | tf_op jit(solution)/shard_map/ppermute | solution.py:28
  117.5 64.1 %collective-permute-start.34 = (f32[128,128]{1,0:T(8,128)S(1)}, f32[128,128]{1,0:T(8,128)}, u32[]{:S(2)}, u32[]{:S(2)}) collective-permute-start(f32[128,128]{1,0:T(8,128)S(1)} %add.225), channel_id=1, source_target_pairs={{0,6},{1,7},{2,8},{3,9},{4,10},{5,11},{6,12},{7,13},{8,14},{9,15},... | collective-permute-start | bytes 196616 | tf_op jit(solution)/shard_map/ppermute | solution.py:28
  178.9 11.3 %collective-permute-start.35 = (f32[128,128]{1,0:T(8,128)S(1)}, f32[128,128]{1,0:T(8,128)S(1)}, u32[]{:S(2)}, u32[]{:S(2)}) collective-permute-start(f32[128,128]{1,0:T(8,128)S(1)} %add.225), channel_id=1, source_target_pairs={{0,4},{1,5},{2,6},{3,7},{4,8},{5,9},{6,10},{7,11},{8,12},{9,13},{1... | collective-permute-start | bytes 196616 | tf_op jit(solution)/shard_map/ppermute | solution.py:28
  181.7 10.9 %collective-permute-start.36 = (f32[128,128]{1,0:T(8,128)S(1)}, f32[128,128]{1,0:T(8,128)S(1)}, u32[]{:S(2)}, u32[]{:S(2)}) collective-permute-start(f32[128,128]{1,0:T(8,128)S(1)} %add.225), channel_id=1, source_target_pairs={{0,2},{1,3},{2,4},{3,5},{4,6},{5,7},{6,8},{7,9},{8,10},{9,11},{10,... | collective-permute-start | bytes 196616 | tf_op jit(solution)/shard_map/ppermute | solution.py:28
  190.2 7.3 collective-permute-start.37
  192.6 8.9 %collective-permute-start.38 = (f32[128,128]{1,0:T(8,128)S(1)}, f32[128,128]{1,0:T(8,128)S(1)}, u32[]{:S(2)}, u32[]{:S(2)}) collective-permute-start(f32[128,128]{1,0:T(8,128)S(1)} %add.225), channel_id=1, source_target_pairs={{4,0},{5,1},{6,2},{7,3},{8,4},{9,5},{10,6},{11,7},{12,8},{13,9},{1... | collective-permute-start | bytes 196616 | tf_op jit(solution)/shard_map/ppermute | solution.py:28
  197.5 9.6 %collective-permute-start.39 = (f32[128,128]{1,0:T(8,128)S(1)}, f32[128,128]{1,0:T(8,128)S(1)}, u32[]{:S(2)}, u32[]{:S(2)}) collective-permute-start(f32[128,128]{1,0:T(8,128)S(1)} %add.225), channel_id=1, source_target_pairs={{6,0},{7,1},{8,2},{9,3},{10,4},{11,5},{12,6},{13,7},{14,8},{15,9},... | collective-permute-start | bytes 196616 | tf_op jit(solution)/shard_map/ppermute | solution.py:28
  201.5 16.3 %collective-permute-start.40 = (f32[128,128]{1,0:T(8,128)S(1)}, f32[128,128]{1,0:T(8,128)S(1)}, u32[]{:S(2)}, u32[]{:S(2)}) collective-permute-start(f32[128,128]{1,0:T(8,128)S(1)} %add.225), channel_id=1, source_target_pairs={{8,0},{9,1},{10,2},{11,3},{12,4},{13,5},{14,6},{15,7},{16,8},{17,9... | collective-permute-start | bytes 196616 | tf_op jit(solution)/shard_map/ppermute | solution.py:28
  207.1 3.1 collective-permute-start.41
  210.2 147.6 %collective-permute-start.3 = (f32[524,128]{1,0:T(8,128)S(1)}, f32[524,128]{1,0:T(8,128)S(1)}, u32[]{:S(2)}, u32[]{:S(2)}) collective-permute-start(f32[524,128]{1,0:T(8,128)S(1)} %pad_maximum_fusion), channel_id=1, source_target_pairs={{0,5},{1,6},{2,7},{3,8},{4,9},{5,10},{6,11},{7,12},{8,13},{9,14},{... | collective-permute-start | bytes 804872 | tf_op jit(solution)/shard_map/ppermute | solution.py:28
  217.8 14.1 %collective-permute-start.42 = (f32[128,128]{1,0:T(8,128)S(1)}, f32[128,128]{1,0:T(8,128)S(1)}, u32[]{:S(2)}, u32[]{:S(2)}) collective-permute-start(f32[128,128]{1,0:T(8,128)S(1)} %add.236), channel_id=1, source_target_pairs={{0,2},{1,3},{2,0},{3,1},{4,6},{5,7},{6,4},{7,5},{8,10},{9,11},{10,... | collective-permute-start | bytes 196616 | tf_op jit(solution)/shard_map/ppermute | solution.py:22
  232.0 19.7 %collective-permute-start.43 = (f32[128,128]{1,0:T(8,128)S(1)}, f32[128,128]{1,0:T(8,128)S(1)}, u32[]{:S(2)}, u32[]{:S(2)}) collective-permute-start(f32[128,128]{1,0:T(8,128)S(1)} %add.237), channel_id=1, source_target_pairs={{0,16},{1,17},{2,18},{3,19},{4,20},{5,21},{6,22},{7,23},{8,24},{9,... | collective-permute-start | bytes 196616 | tf_op jit(solution)/shard_map/ppermute | solution.py:28
  251.7 16.1 %collective-permute-start.44 = (f32[128,128]{1,0:T(8,128)S(1)}, f32[128,128]{1,0:T(8,128)S(1)}, u32[]{:S(2)}, u32[]{:S(2)}) collective-permute-start(f32[128,128]{1,0:T(8,128)S(1)} %add.237), channel_id=1, source_target_pairs={{0,12},{1,13},{2,14},{3,15},{4,16},{5,17},{6,18},{7,19},{8,20},{9,... | collective-permute-start | bytes 196616 | tf_op jit(solution)/shard_map/ppermute | solution.py:28
  267.8 13.1 %collective-permute-start.45 = (f32[128,128]{1,0:T(8,128)S(1)}, f32[128,128]{1,0:T(8,128)S(1)}, u32[]{:S(2)}, u32[]{:S(2)}) collective-permute-start(f32[128,128]{1,0:T(8,128)S(1)} %add.237), channel_id=1, source_target_pairs={{0,8},{1,9},{2,10},{3,11},{4,12},{5,13},{6,14},{7,15},{8,16},{9,17... | collective-permute-start | bytes 196616 | tf_op jit(solution)/shard_map/ppermute | solution.py:28
  280.8 11.3 %collective-permute-start.46 = (f32[128,128]{1,0:T(8,128)S(1)}, f32[128,128]{1,0:T(8,128)S(1)}, u32[]{:S(2)}, u32[]{:S(2)}) collective-permute-start(f32[128,128]{1,0:T(8,128)S(1)} %add.237), channel_id=1, source_target_pairs={{0,4},{1,5},{2,6},{3,7},{4,8},{5,9},{6,10},{7,11},{8,12},{9,13},{1... | collective-permute-start | bytes 196616 | tf_op jit(solution)/shard_map/ppermute | solution.py:28
  292.1 7.1 collective-permute-start.47
  299.2 10.1 %collective-permute-start.48 = (f32[128,128]{1,0:T(8,128)S(1)}, f32[128,128]{1,0:T(8,128)S(1)}, u32[]{:S(2)}, u32[]{:S(2)}) collective-permute-start(f32[128,128]{1,0:T(8,128)S(1)} %add.237), channel_id=1, source_target_pairs={{8,0},{9,1},{10,2},{11,3},{12,4},{13,5},{14,6},{15,7},{16,8},{17,9... | collective-permute-start | bytes 196616 | tf_op jit(solution)/shard_map/ppermute | solution.py:28
  309.2 11.9 %collective-permute-start.49 = (f32[128,128]{1,0:T(8,128)S(1)}, f32[128,128]{1,0:T(8,128)S(1)}, u32[]{:S(2)}, u32[]{:S(2)}) collective-permute-start(f32[128,128]{1,0:T(8,128)S(1)} %add.237), channel_id=1, source_target_pairs={{12,0},{13,1},{14,2},{15,3},{16,4},{17,5},{18,6},{19,7},{20,8},{21... | collective-permute-start | bytes 196616 | tf_op jit(solution)/shard_map/ppermute | solution.py:28
  321.1 16.2 %collective-permute-start.50 = (f32[128,128]{1,0:T(8,128)S(1)}, f32[128,128]{1,0:T(8,128)S(1)}, u32[]{:S(2)}, u32[]{:S(2)}) collective-permute-start(f32[128,128]{1,0:T(8,128)S(1)} %add.237), channel_id=1, source_target_pairs={{16,0},{17,1},{18,2},{19,3},{20,4},{21,5},{22,6},{23,7},{24,8},{25... | collective-permute-start | bytes 196616 | tf_op jit(solution)/shard_map/ppermute | solution.py:28
  337.3 3.3 collective-permute-start.51
  340.6 28.6 %collective-permute-start.4 = (f32[524,128]{1,0:T(8,128)S(1)}, f32[524,128]{1,0:T(8,128)S(1)}, u32[]{:S(2)}, u32[]{:S(2)}) collective-permute-start(f32[524,128]{1,0:T(8,128)S(1)} %pad_maximum_fusion), channel_id=1, source_target_pairs={{0,4},{1,5},{2,6},{3,7},{4,8},{5,9},{6,10},{7,11},{8,12},{9,13},{1... | collective-permute-start | bytes 804872 | tf_op jit(solution)/shard_map/ppermute | solution.py:28
  343.9 32.4 %collective-permute-start.5 = (f32[524,128]{1,0:T(8,128)S(1)}, f32[524,128]{1,0:T(8,128)S(1)}, u32[]{:S(2)}, u32[]{:S(2)}) collective-permute-start(f32[524,128]{1,0:T(8,128)S(1)} %pad_maximum_fusion), channel_id=1, source_target_pairs={{0,3},{1,4},{2,5},{3,6},{4,7},{5,8},{6,9},{7,10},{8,11},{9,12},{10... | collective-permute-start | bytes 804872 | tf_op jit(solution)/shard_map/ppermute | solution.py:28
  349.4 34.0 %collective-permute-start.6 = (f32[524,128]{1,0:T(8,128)S(1)}, f32[524,128]{1,0:T(8,128)S(1)}, u32[]{:S(2)}, u32[]{:S(2)}) collective-permute-start(f32[524,128]{1,0:T(8,128)S(1)} %pad_maximum_fusion), channel_id=1, source_target_pairs={{0,2},{1,3},{2,4},{3,5},{4,6},{5,7},{6,8},{7,9},{8,10},{9,11},{10,... | collective-permute-start | bytes 804872 | tf_op jit(solution)/shard_map/ppermute | solution.py:28
  352.5 36.9 %collective-permute-start.7 = (f32[524,128]{1,0:T(8,128)S(1)}, f32[524,128]{1,0:T(8,128)S(1)}, u32[]{:S(2)}, u32[]{:S(2)}) collective-permute-start(f32[524,128]{1,0:T(8,128)S(1)} %pad_maximum_fusion), channel_id=1, source_target_pairs={{0,1},{1,2},{2,3},{3,4},{4,5},{5,6},{6,7},{7,8},{8,9},{9,10},{10,1... | collective-permute-start | bytes 804872 | tf_op jit(solution)/shard_map/ppermute | solution.py:28
  357.7 328.5 %copy-start.8 = (f32[1024]{0:T(1024)S(1)}, f32[1024]{0:T(1024)}, u32[]{:S(2)}) copy-start(f32[1024]{0:T(1024)} %get-tuple-element.101) | copy-start | bytes 12292
  357.7 328.5 %copy-start.9 = (f32[1024]{0:T(1024)S(1)}, f32[1024]{0:T(1024)}, u32[]{:S(2)}) copy-start(f32[1024]{0:T(1024)} %get-tuple-element.102) | copy-start | bytes 12292
  357.7 328.5 %copy-start.17 = (f32[128]{0:T(128)S(1)}, f32[128]{0:T(128)}, u32[]{:S(2)}) copy-start(f32[128]{0:T(128)} %get-tuple-element.94) | copy-start | bytes 1540
  357.7 328.5 %copy-start.18 = (f32[128]{0:T(128)S(1)}, f32[128]{0:T(128)}, u32[]{:S(2)}) copy-start(f32[128]{0:T(128)} %get-tuple-element.95) | copy-start | bytes 1540
  357.7 328.5 %copy-start.19 = (f32[128]{0:T(128)S(1)}, f32[128]{0:T(128)}, u32[]{:S(2)}) copy-start(f32[128]{0:T(128)} %get-tuple-element.96) | copy-start | bytes 1540
  357.8 328.5 %copy-start.22 = (pred[1024]{0:T(1024)(128)(4,1)S(1)}, pred[1024]{0:T(1024)(128)(4,1)}, u32[]{:S(2)}) copy-start(pred[1024]{0:T(1024)(128)(4,1)} %broadcast_bitcast_fusion) | copy-start | bytes 3076
  357.8 328.5 %copy-start.23 = (pred[1024]{0:T(1024)(128)(4,1)S(1)}, pred[1024]{0:T(1024)(128)(4,1)}, u32[]{:S(2)}) copy-start(pred[1024]{0:T(1024)(128)(4,1)} %broadcast_bitcast_fusion.1) | copy-start | bytes 3076
  357.8 35.0 %collective-permute-start.8 = (f32[524,128]{1,0:T(8,128)S(1)}, f32[524,128]{1,0:T(8,128)S(1)}, u32[]{:S(2)}, u32[]{:S(2)}) collective-permute-start(f32[524,128]{1,0:T(8,128)S(1)} %pad_maximum_fusion), channel_id=1, source_target_pairs={{1,0},{2,1},{3,2},{4,3},{5,4},{6,5},{7,6},{8,7},{9,8},{10,9},{11,1... | collective-permute-start | bytes 804872 | tf_op jit(solution)/shard_map/ppermute | solution.py:28
  369.2 26.4 %collective-permute-start.9 = (f32[524,128]{1,0:T(8,128)S(1)}, f32[524,128]{1,0:T(8,128)S(1)}, u32[]{:S(2)}, u32[]{:S(2)}) collective-permute-start(f32[524,128]{1,0:T(8,128)S(1)} %pad_maximum_fusion), channel_id=1, source_target_pairs={{2,0},{3,1},{4,2},{5,3},{6,4},{7,5},{8,6},{9,7},{10,8},{11,9},{12,... | collective-permute-start | bytes 804872 | tf_op jit(solution)/shard_map/ppermute | solution.py:28
  376.3 21.9 %collective-permute-start.10 = (f32[524,128]{1,0:T(8,128)S(1)}, f32[524,128]{1,0:T(8,128)S(1)}, u32[]{:S(2)}, u32[]{:S(2)}) collective-permute-start(f32[524,128]{1,0:T(8,128)S(1)} %pad_maximum_fusion), channel_id=1, source_target_pairs={{3,0},{4,1},{5,2},{6,3},{7,4},{8,5},{9,6},{10,7},{11,8},{12,9},{13... | collective-permute-start | bytes 804872 | tf_op jit(solution)/shard_map/ppermute | solution.py:28
  383.4 28.6 %collective-permute-start.11 = (f32[524,128]{1,0:T(8,128)S(1)}, f32[524,128]{1,0:T(8,128)S(1)}, u32[]{:S(2)}, u32[]{:S(2)}) collective-permute-start(f32[524,128]{1,0:T(8,128)S(1)} %pad_maximum_fusion), channel_id=1, source_target_pairs={{4,0},{5,1},{6,2},{7,3},{8,4},{9,5},{10,6},{11,7},{12,8},{13,9},{1... | collective-permute-start | bytes 804872 | tf_op jit(solution)/shard_map/ppermute | solution.py:28
  389.5 33.5 %collective-permute-start.12 = (f32[524,128]{1,0:T(8,128)S(1)}, f32[524,128]{1,0:T(8,128)S(1)}, u32[]{:S(2)}, u32[]{:S(2)}) collective-permute-start(f32[524,128]{1,0:T(8,128)S(1)} %pad_maximum_fusion), channel_id=1, source_target_pairs={{5,0},{6,1},{7,2},{8,3},{9,4},{10,5},{11,6},{12,7},{13,8},{14,9},{... | collective-permute-start | bytes 804872 | tf_op jit(solution)/shard_map/ppermute | solution.py:28
  392.8 87.4 %collective-permute-start.13 = (f32[524,128]{1,0:T(8,128)S(1)}, f32[524,128]{1,0:T(8,128)S(1)}, u32[]{:S(2)}, u32[]{:S(2)}) collective-permute-start(f32[524,128]{1,0:T(8,128)S(1)} %pad_maximum_fusion), channel_id=1, source_target_pairs={{6,0},{7,1},{8,2},{9,3},{10,4},{11,5},{12,6},{13,7},{14,8},{15,9},... | collective-permute-start | bytes 804872 | tf_op jit(solution)/shard_map/ppermute | solution.py:28
  395.6 307.8 %collective-permute-start.14 = (f32[524,128]{1,0:T(8,128)S(1)}, f32[524,128]{1,0:T(8,128)S(1)}, u32[]{:S(2)}, u32[]{:S(2)}) collective-permute-start(f32[524,128]{1,0:T(8,128)S(1)} %pad_maximum_fusion), channel_id=1, source_target_pairs={{7,0},{8,1},{9,2},{10,3},{11,4},{12,5},{13,6},{14,7},{15,8},{16,9}... | collective-permute-start | bytes 804872 | tf_op jit(solution)/shard_map/ppermute | solution.py:28
  398.3 307.9 %collective-permute-start.15 = (f32[524,128]{1,0:T(8,128)S(1)}, f32[524,128]{1,0:T(8,128)S(1)}, u32[]{:S(2)}, u32[]{:S(2)}) collective-permute-start(f32[524,128]{1,0:T(8,128)S(1)} %pad_maximum_fusion), channel_id=1, source_target_pairs={{8,0},{9,1},{10,2},{11,3},{12,4},{13,5},{14,6},{15,7},{16,8},{17,9... | collective-permute-start | bytes 804872 | tf_op jit(solution)/shard_map/ppermute | solution.py:28
  412.0 66.3 %collective-permute-start.52 = (f32[128,128]{0,1:T(8,128)S(1)}, f32[128,128]{0,1:T(8,128)S(1)}, u32[]{:S(2)}, u32[]{:S(2)}) collective-permute-start(f32[128,128]{0,1:T(8,128)S(1)} %add.244), channel_id=1, source_target_pairs={{0,2},{1,3},{2,0},{3,1},{4,6},{5,7},{6,4},{7,5},{8,10},{9,11},{10,... | collective-permute-start | bytes 196616 | tf_op jit(solution)/shard_map/ppermute | solution.py:22
  478.4 7.1 collective-permute-start.53
  701.2 3.1 collective-permute-start.54
  704.3 5.8 collective-permute-start.55
  710.3 79.4 %collective-permute-start.56 = (f32[64,128]{1,0:T(8,128)S(1)}, f32[64,128]{1,0:T(8,128)S(1)}, u32[]{:S(2)}, u32[]{:S(2)}) collective-permute-start(f32[64,128]{1,0:T(8,128)S(1)} %fusion.26), channel_id=1, source_target_pairs={{0,1},{1,0},{2,3},{3,2},{4,5},{5,4},{6,7},{7,6},{8,9},{9,8},{10,11... | collective-permute-start | bytes 98312 | tf_op jit(solution)/shard_map/ppermute | solution.py:22
  (17 other events, 2806.1 us)

commit v2 on v1

--- a/solution.py
+++ b/solution.py
@@ -114,6 +114,33 @@
         transfer_rows, above, precision=HIGHEST
     )
     return join_rows(rows_here, stride.bit_length() - 1, device)
+
+
+def cluster_gather(block, device, clusters):
+    gathered = block[None]
+    for level in range(clusters.bit_length() - 1):
+        bit_index = 3 + level
+        other = from_partner(gathered, AX, bit_index)
+        upper = device // 2**bit_index % 2
+        gathered = jnp.where(
+            upper == 0,
+            jnp.concatenate([gathered, other], 0),
+            jnp.concatenate([other, gathered], 0),
+        )
+    return gathered
+
+
+def near_sum(own_points, near_entries, shipped, device):
+    leaf_points = own_points.shape[1]
+    total = None
+    for distance in range(-REACH, REACH + 1):
+        block = shipped if distance == 0 else from_behind(shipped, AX, -distance)
+        listed = jnp.any(near_entries == device + distance)
+        coords = block[leaf_points:].reshape(3, leaf_points)
+        contrib = jnp.dot(kernel_block(own_points, coords), block[:leaf_points], precision=HIGHEST)
+        contrib = jnp.where(listed, contrib, 0.0)
+        total = contrib if total is None else total + contrib
+    return total
 
 
 def per_device(
@@ -141,14 +168,7 @@
     shipped = jnp.concatenate(
         [vectors[0], own_points.reshape(3 * leaf_points // width, width)], axis=0
     )
-    near_rim = window(shipped)
-
-    def near_fetch(partner):
-        position = jnp.clip(partner - device + REACH, 0, 2 * REACH)
-        block = lax.dynamic_index_in_dim(near_rim, position, 0, keepdims=False)
-        return (block[leaf_points:].reshape(3, leaf_points), block[:leaf_points])
-
-    near_field = listed_sum(own_points, near_list[0], near_fetch, width)
+    near_field = near_sum(own_points, near_list[0], shipped, device)
     coef_leaf = transposed_dot(leaf_basis[0], vectors[0])
     coef_pair = pair_total(transposed_dot(transfer_leaf[0], coef_leaf), 1)
     pair_rows = lax.dynamic_slice_in_dim(coef_pair, device % 2 * (rank // 2), rank // 2, 0)
@@ -159,7 +179,7 @@
     top_member = device % 8
     share = width // 8
     top_cols_own = lax.dynamic_slice_in_dim(coef_top, top_member * share, share, 1)
-    all_top = lax.all_gather(top_cols_own, "cl", axis=0)
+    all_top = cluster_gather(top_cols_own, device, lax.axis_size("cl"))
     top_coords = lax.dynamic_index_in_dim(skel_top, top_cluster, 0, keepdims=False)
     top_entries = lax.dynamic_index_in_dim(far_top, top_cluster, 0, keepdims=False)
     top_chosen = jnp.maximum(top_entries, 0)

time: 804 us -> 519 us (0.65); the launches traced: 791 us -> 514 us
  blocking collectives: 214 us -> 14 us
  waiting for transfers between devices: 236 us -> 158 us
  starting transfers between devices: 210 us -> 282 us
  local copies, waits for them, and re-layouts: 53.3 us -> 8.42 us
  loops' own time: 18.3 us -> 0 us
    all_gather x1 -> x0, blocking collectives: 200 us -> none  [per_device(): all_top = lax.all_gather(top_cols_own, 'cl', axis=0)]
    ppermute x48, waiting for transfers between devices: 162 us -> 101 us  [from_behind(): return lax.ppermute(block, axis, route)]
    ppermute x48, starting transfers between devices: 192 us -> 246 us  [from_behind(): return lax.ppermute(block, axis, route)]
    ppermute x9 -> x15, starting transfers between devices: 17.6 us -> 36.3 us  [from_partner(): return lax.ppermute(value, axis, pairs)]
    another operation x1 -> x0, loops' own time: 18.3 us -> none  [listed_sum(): result, _ = lax.scan(advance, start_value, entries)]
    sub x23, local copies, waits for them, and re-layouts: 18.9 us -> 1.74 us  [kernel_block(): offset_gap = left_pts[axis_id][:, None] - right_pts[axis_id][None, :]]
    ppermute x9 -> x15, waiting for transfers between devices: 73.6 us -> 56.7 us  [from_partner(): return lax.ppermute(value, axis, pairs)]
    unnamed x95 -> x73, local copies, waits for them, and re-layouts: 15.3 us -> 1.46 us
  transfers between devices with their start and end apart: 57 -> 63, of which waited for: 21 -> 28; matrix products, arithmetic and copies ran while one was open for 14% -> 10% of each run, Pallas kernels for 0% -> 0%
where the time goes in v2:
time: 519 us; the launch traced here: 514 us
  starting transfers between devices  282 us (54%)
  waiting for transfers between devices  158 us (30%)
  matrix products  46.9 us (9%)
  blocking collectives  14 us (3%)
  local copies, waits for them, and re-layouts  8.42 us (2%)
    ppermute x48, starting transfers between devices, from_behind(): return lax.ppermute(block, axis, route)  246 us
    ppermute x48, waiting for transfers between devices, from_behind(): return lax.ppermute(block, axis, route)  101 us
    ppermute x15, waiting for transfers between devices, from_partner(): return lax.ppermute(value, axis, pairs)  56.7 us
    dot_general x17, matrix products, near_sum(): jnp.dot(kernel_block(own_points, coords), block[:leaf_points], precision=...  40 us
    ppermute x15, starting transfers between devices, from_partner(): return lax.ppermute(value, axis, pairs)  36.3 us
    all_gather x1, blocking collectives, per_device(): local_top = lax.all_gather(top_cols, MEMBERS, axis=1, tiled=True)  14 us
  transfers between devices with their start and end apart: 63, of which 28 were waited for; matrix products, arithmetic and copies ran while one was open for 10% of the time, Pallas kernels for 0%

profile of v2, /device:TPU:24, one launch (start us, length us, event | category | flops | bytes accessed | tf_op | source)
XLA Modules:
  0.0 514.2 jit_solution(862871679871508502)
XLA Ops:
  2.7 9.1 %collective-permute-start.16 = (f32[131,128]{1,0:T(8,128)S(1)}, f32[131,128]{1,0:T(8,128)S(1)}, u32[]{:S(2)}, u32[]{:S(2)}) collective-permute-start(f32[131,128]{1,0:T(8,128)S(1)} %pad_maximum_fusion.1), channel_id=1, source_target_pairs={{0,8},{1,9},{2,10},{3,11},{4,12},{5,13},{6,14},{7,15},{8,16},{9,17... | collective-permute-start | bytes 201224 | tf_op jit(solution)/shard_map/ppermute | solution.py:28
  11.8 5.7 %collective-permute-start.17 = (f32[131,128]{1,0:T(8,128)S(1)}, f32[131,128]{1,0:T(8,128)S(1)}, u32[]{:S(2)}, u32[]{:S(2)}) collective-permute-start(f32[131,128]{1,0:T(8,128)S(1)} %pad_maximum_fusion.1), channel_id=1, source_target_pairs={{0,7},{1,8},{2,9},{3,10},{4,11},{5,12},{6,13},{7,14},{8,15},{9,16}... | collective-permute-start | bytes 201224 | tf_op jit(solution)/shard_map/ppermute | solution.py:28
  17.5 5.9 %collective-permute-start.18 = (f32[131,128]{1,0:T(8,128)S(1)}, f32[131,128]{1,0:T(8,128)S(1)}, u32[]{:S(2)}, u32[]{:S(2)}) collective-permute-start(f32[131,128]{1,0:T(8,128)S(1)} %pad_maximum_fusion.1), channel_id=1, source_target_pairs={{0,6},{1,7},{2,8},{3,9},{4,10},{5,11},{6,12},{7,13},{8,14},{9,15},... | collective-permute-start | bytes 201224 | tf_op jit(solution)/shard_map/ppermute | solution.py:28
  23.5 4.1 collective-permute-start.19
  36.7 2.7 convolution_select_fusion.8
  40.2 3.4 collective-permute-start.20
  50.8 7.5 %collective-permute-start.24 = (f32[131,128]{1,0:T(8,128)S(1)}, f32[131,128]{1,0:T(8,128)S(1)}, u32[]{:S(2)}, u32[]{:S(2)}) collective-permute-start(f32[131,128]{1,0:T(8,128)S(1)} %pad_maximum_fusion.1), channel_id=1, source_target_pairs={{1,0},{2,1},{3,2},{4,3},{5,4},{6,5},{7,6},{8,7},{9,8},{10,9},{11,1... | collective-permute-start | bytes 201224 | tf_op jit(solution)/shard_map/ppermute | solution.py:28
  58.3 3.3 collective-permute-start.25
  61.6 2.9 collective-permute-start.26
  64.6 4.6 collective-permute-start.27
  69.2 4.1 collective-permute-start.28
  73.3 4.0 collective-permute-start.29
  79.6 5.7 %collective-permute-start.31 = (f32[131,128]{1,0:T(8,128)S(1)}, f32[131,128]{1,0:T(8,128)S(1)}, u32[]{:S(2)}, u32[]{:S(2)}) collective-permute-start(f32[131,128]{1,0:T(8,128)S(1)} %pad_maximum_fusion.1), channel_id=1, source_target_pairs={{8,0},{9,1},{10,2},{11,3},{12,4},{13,5},{14,6},{15,7},{16,8},{17,9... | collective-permute-start | bytes 201224 | tf_op jit(solution)/shard_map/ppermute | solution.py:28
  90.0 4.1 collective-permute-start.4
  94.1 7.5 %collective-permute-start.33 = (f32[128,128]{1,0:T(8,128)S(1)}, f32[128,128]{1,0:T(8,128)S(1)}, u32[]{:S(2)}, u32[]{:S(2)}) collective-permute-start(f32[128,128]{1,0:T(8,128)S(1)} %add.560), channel_id=1, source_target_pairs={{0,8},{1,9},{2,10},{3,11},{4,12},{5,13},{6,14},{7,15},{8,16},{9,17... | collective-permute-start | bytes 196616 | tf_op jit(solution)/shard_map/ppermute | solution.py:28
  106.1 10.5 %collective-permute-done.33 = f32[128,128]{1,0:T(8,128)S(1)} collective-permute-done((f32[128,128]{1,0:T(8,128)S(1)}, f32[128,128]{1,0:T(8,128)S(1)}, u32[]{:S(2)}, u32[]{:S(2)}) %collective-permute-start.33) | collective-permute-done | bytes 65568 | tf_op jit(solution)/shard_map/ppermute | solution.py:28
  116.5 5.6 %collective-permute-start.35 = (f32[128,128]{1,0:T(8,128)S(1)}, f32[128,128]{1,0:T(8,128)S(1)}, u32[]{:S(2)}, u32[]{:S(2)}) collective-permute-start(f32[128,128]{1,0:T(8,128)S(1)} %add.560), channel_id=1, source_target_pairs={{0,4},{1,5},{2,6},{3,7},{4,8},{5,9},{6,10},{7,11},{8,12},{9,13},{1... | collective-permute-start | bytes 196616 | tf_op jit(solution)/shard_map/ppermute | solution.py:28
  122.2 3.2 collective-permute-done.34
  125.4 13.1 %collective-permute-start.36 = (f32[128,128]{1,0:T(8,128)S(1)}, f32[128,128]{1,0:T(8,128)S(1)}, u32[]{:S(2)}, u32[]{:S(2)}) collective-permute-start(f32[128,128]{1,0:T(8,128)S(1)} %add.560), channel_id=1, source_target_pairs={{0,2},{1,3},{2,4},{3,5},{4,6},{5,7},{6,8},{7,9},{8,10},{9,11},{10,... | collective-permute-start | bytes 196616 | tf_op jit(solution)/shard_map/ppermute | solution.py:28
  140.6 3.6 collective-permute-start.38
  145.8 3.1 collective-permute-start.39
  148.9 5.1 %collective-permute-start.40 = (f32[128,128]{1,0:T(8,128)S(1)}, f32[128,128]{1,0:T(8,128)S(1)}, u32[]{:S(2)}, u32[]{:S(2)}) collective-permute-start(f32[128,128]{1,0:T(8,128)S(1)} %add.560), channel_id=1, source_target_pairs={{8,0},{9,1},{10,2},{11,3},{12,4},{13,5},{14,6},{15,7},{16,8},{17,9... | collective-permute-start | bytes 196616 | tf_op jit(solution)/shard_map/ppermute | solution.py:28
  159.3 4.0 collective-permute-start.3
  163.3 5.0 collective-permute-start.42
  169.6 6.1 %collective-permute-done.42 = f32[128,128]{1,0:T(8,128)S(1)} collective-permute-done((f32[128,128]{1,0:T(8,128)S(1)}, f32[128,128]{1,0:T(8,128)S(1)}, u32[]{:S(2)}, u32[]{:S(2)}) %collective-permute-start.42) | collective-permute-done | bytes 65568 | tf_op jit(solution)/shard_map/ppermute | solution.py:22
  175.8 10.8 %collective-permute-start.43 = (f32[128,128]{1,0:T(8,128)S(1)}, f32[128,128]{1,0:T(8,128)S(1)}, u32[]{:S(2)}, u32[]{:S(2)}) collective-permute-start(f32[128,128]{1,0:T(8,128)S(1)} %add.572), channel_id=1, source_target_pairs={{0,16},{1,17},{2,18},{3,19},{4,20},{5,21},{6,22},{7,23},{8,24},{9,... | collective-permute-start | bytes 196616 | tf_op jit(solution)/shard_map/ppermute | solution.py:28
  186.8 7.0 %collective-permute-done.43 = f32[128,128]{1,0:T(8,128)S(1)} collective-permute-done((f32[128,128]{1,0:T(8,128)S(1)}, f32[128,128]{1,0:T(8,128)S(1)}, u32[]{:S(2)}, u32[]{:S(2)}) %collective-permute-start.43) | collective-permute-done | bytes 65568 | tf_op jit(solution)/shard_map/ppermute | solution.py:28
  193.8 13.4 %collective-permute-start.44 = (f32[128,128]{1,0:T(8,128)S(1)}, f32[128,128]{1,0:T(8,128)S(1)}, u32[]{:S(2)}, u32[]{:S(2)}) collective-permute-start(f32[128,128]{1,0:T(8,128)S(1)} %add.572), channel_id=1, source_target_pairs={{0,12},{1,13},{2,14},{3,15},{4,16},{5,17},{6,18},{7,19},{8,20},{9,... | collective-permute-start | bytes 196616 | tf_op jit(solution)/shard_map/ppermute | solution.py:28
  207.3 3.3 collective-permute-done.44
  210.6 13.2 %collective-permute-start.45 = (f32[128,128]{1,0:T(8,128)S(1)}, f32[128,128]{1,0:T(8,128)S(1)}, u32[]{:S(2)}, u32[]{:S(2)}) collective-permute-start(f32[128,128]{1,0:T(8,128)S(1)} %add.572), channel_id=1, source_target_pairs={{0,8},{1,9},{2,10},{3,11},{4,12},{5,13},{6,14},{7,15},{8,16},{9,17... | collective-permute-start | bytes 196616 | tf_op jit(solution)/shard_map/ppermute | solution.py:28
  225.7 4.5 collective-permute-start.46
  230.2 6.7 %collective-permute-done.46 = f32[128,128]{1,0:T(8,128)S(1)} collective-permute-done((f32[128,128]{1,0:T(8,128)S(1)}, f32[128,128]{1,0:T(8,128)S(1)}, u32[]{:S(2)}, u32[]{:S(2)}) %collective-permute-start.46) | collective-permute-done | bytes 65568 | tf_op jit(solution)/shard_map/ppermute | solution.py:28
  238.9 5.1 collective-permute-done.47
  245.9 9.1 %collective-permute-done.48 = f32[128,128]{1,0:T(8,128)S(1)} collective-permute-done((f32[128,128]{1,0:T(8,128)S(1)}, f32[128,128]{1,0:T(8,128)S(1)}, u32[]{:S(2)}, u32[]{:S(2)}) %collective-permute-start.48) | collective-permute-done | bytes 65568 | tf_op jit(solution)/shard_map/ppermute | solution.py:28
  255.0 6.2 %collective-permute-start.49 = (f32[128,128]{1,0:T(8,128)S(1)}, f32[128,128]{1,0:T(8,128)S(1)}, u32[]{:S(2)}, u32[]{:S(2)}) collective-permute-start(f32[128,128]{1,0:T(8,128)S(1)} %add.572), channel_id=1, source_target_pairs={{12,0},{13,1},{14,2},{15,3},{16,4},{17,5},{18,6},{19,7},{20,8},{21... | collective-permute-start | bytes 196616 | tf_op jit(solution)/shard_map/ppermute | solution.py:28
  261.2 9.6 %collective-permute-done.49 = f32[128,128]{1,0:T(8,128)S(1)} collective-permute-done((f32[128,128]{1,0:T(8,128)S(1)}, f32[128,128]{1,0:T(8,128)S(1)}, u32[]{:S(2)}, u32[]{:S(2)}) %collective-permute-start.49) | collective-permute-done | bytes 65568 | tf_op jit(solution)/shard_map/ppermute | solution.py:28
  270.8 7.4 %collective-permute-start.50 = (f32[128,128]{1,0:T(8,128)S(1)}, f32[128,128]{1,0:T(8,128)S(1)}, u32[]{:S(2)}, u32[]{:S(2)}) collective-permute-start(f32[128,128]{1,0:T(8,128)S(1)} %add.572), channel_id=1, source_target_pairs={{16,0},{17,1},{18,2},{19,3},{20,4},{21,5},{22,6},{23,7},{24,8},{25... | collective-permute-start | bytes 196616 | tf_op jit(solution)/shard_map/ppermute | solution.py:28
  278.2 7.6 %collective-permute-done.50 = f32[128,128]{1,0:T(8,128)S(1)} collective-permute-done((f32[128,128]{1,0:T(8,128)S(1)}, f32[128,128]{1,0:T(8,128)S(1)}, u32[]{:S(2)}, u32[]{:S(2)}) %collective-permute-start.50) | collective-permute-done | bytes 65568 | tf_op jit(solution)/shard_map/ppermute | solution.py:28
  289.0 7.7 %collective-permute-start.2 = (f32[524,128]{1,0:T(8,128)S(1)}, f32[524,128]{1,0:T(8,128)S(1)}, u32[]{:S(2)}, u32[]{:S(2)}) collective-permute-start(f32[524,128]{1,0:T(8,128)S(1)} %pad_maximum_fusion), channel_id=1, source_target_pairs={{0,6},{1,7},{2,8},{3,9},{4,10},{5,11},{6,12},{7,13},{8,14},{9,15},... | collective-permute-start | bytes 804872 | tf_op jit(solution)/shard_map/ppermute | solution.py:28
  296.7 2.7 collective-permute-start.1
  299.4 4.2 collective-permute-start.7
  306.4 10.7 %collective-permute-start.15 = (f32[524,128]{1,0:T(8,128)S(1)}, f32[524,128]{1,0:T(8,128)S(1)}, u32[]{:S(2)}, u32[]{:S(2)}) collective-permute-start(f32[524,128]{1,0:T(8,128)S(1)} %pad_maximum_fusion), channel_id=1, source_target_pairs={{8,0},{9,1},{10,2},{11,3},{12,4},{13,5},{14,6},{15,7},{16,8},{17,9... | collective-permute-start | bytes 804872 | tf_op jit(solution)/shard_map/ppermute | solution.py:28
  317.2 4.9 collective-permute-done.2
  322.1 15.8 %collective-permute-start.14 = (f32[524,128]{1,0:T(8,128)S(1)}, f32[524,128]{1,0:T(8,128)S(1)}, u32[]{:S(2)}, u32[]{:S(2)}) collective-permute-start(f32[524,128]{1,0:T(8,128)S(1)} %pad_maximum_fusion), channel_id=1, source_target_pairs={{7,0},{8,1},{9,2},{10,3},{11,4},{12,5},{13,6},{14,7},{15,8},{16,9}... | collective-permute-start | bytes 804872 | tf_op jit(solution)/shard_map/ppermute | solution.py:28
  337.9 26.1 %collective-permute-done.1 = f32[524,128]{1,0:T(8,128)S(1)} collective-permute-done((f32[524,128]{1,0:T(8,128)S(1)}, f32[524,128]{1,0:T(8,128)S(1)}, u32[]{:S(2)}, u32[]{:S(2)}) %collective-permute-start.1) | collective-permute-done | bytes 268320 | tf_op jit(solution)/shard_map/ppermute | solution.py:28
  372.5 4.2 collective-permute-start.10
  380.6 2.9 convolution_select_fusion.12
  393.2 2.9 fusion.17
  396.2 3.4 collective-permute-start.52
  402.2 10.8 %collective-permute-done.52 = f32[128,128]{0,1:T(8,128)S(1)} collective-permute-done((f32[128,128]{0,1:T(8,128)S(1)}, f32[128,128]{0,1:T(8,128)S(1)}, u32[]{:S(2)}, u32[]{:S(2)}) %collective-permute-start.52) | collective-permute-done | bytes 65568 | tf_op jit(solution)/shard_map/ppermute | solution.py:22
  413.0 4.3 collective-permute-start.9
  419.3 5.8 %collective-permute-done.53 = f32[128,128]{0,1:T(8,128)S(1)} collective-permute-done((f32[128,128]{0,1:T(8,128)S(1)}, f32[128,128]{0,1:T(8,128)S(1)}, u32[]{:S(2)}, u32[]{:S(2)}) %collective-permute-start.53) | collective-permute-done | bytes 65568 | tf_op jit(solution)/shard_map/ppermute | solution.py:22
  427.0 2.6 convolution_select_fusion.2
  429.7 4.9 collective-permute-done.54
  434.6 4.1 collective-permute-start.8
  440.6 12.4 %collective-permute-done.55 = f32[2,128,16]{1,2,0:T(8,128)S(1)} collective-permute-done((f32[2,128,16]{1,2,0:T(8,128)S(1)}, f32[2,128,16]{1,2,0:T(8,128)S(1)}, u32[]{:S(2)}, u32[]{:S(2)}) %collective-permute-start.55) | collective-permute-done | bytes 16416 | tf_op jit(solution)/shard_map/ppermute | solution.py:22
  454.9 2.7 convolution_select_fusion.3
  460.8 5.7 %collective-permute-done.57 = f32[8,128,16]{1,2,0:T(8,128)S(1)} collective-permute-done((f32[8,128,16]{1,2,0:T(8,128)S(1)}, f32[8,128,16]{1,2,0:T(8,128)S(1)}, u32[]{:S(2)}, u32[]{:S(2)}) %collective-permute-start.57) | collective-permute-done | bytes 65568 | tf_op jit(solution)/shard_map/ppermute | solution.py:22
  466.5 3.5 collective-permute-start.58
  473.4 3.1 collective-permute-start.59
  476.5 2.7 convolution_select_fusion.5
  479.2 4.0 collective-permute-done.59
  484.5 14.0 %all_gather.3 = f32[128,128]{0,1:T(8,128)S(1)} all-gather(f32[128,16]{0,1:T(8,128)S(1)} %fusion.208), channel_id=1, replica_groups=mesh['cl'=64,'q'=2,'p'=2,'c'=2] {'q','p','c'}, dimensions={1}, use_global_device_ids=true | all-gather | bytes 73728 | tf_op jit(solution)/shard_map/all_gather | solution.py:192
  511.6 2.7 fusion.9
  (247 shorter events, 105.4 us)
Async XLA Ops:
  0.0 35.7 %copy-start.1 = (f32[1,512,128]{2,1,0:T(8,128)S(1)}, f32[1,512,128]{2,1,0:T(8,128)}, u32[]{:S(2)}) copy-start(f32[1,512,128]{2,1,0:T(8,128)} %param.17) | copy-start | bytes 786436
  2.7 41.2 %collective-permute-start.16 = (f32[131,128]{1,0:T(8,128)S(1)}, f32[131,128]{1,0:T(8,128)S(1)}, u32[]{:S(2)}, u32[]{:S(2)}) collective-permute-start(f32[131,128]{1,0:T(8,128)S(1)} %pad_maximum_fusion.1), channel_id=1, source_target_pairs={{0,8},{1,9},{2,10},{3,11},{4,12},{5,13},{6,14},{7,15},{8,16},{9,17... | collective-permute-start | bytes 201224 | tf_op jit(solution)/shard_map/ppermute | solution.py:28
  11.8 34.0 %collective-permute-start.17 = (f32[131,128]{1,0:T(8,128)S(1)}, f32[131,128]{1,0:T(8,128)S(1)}, u32[]{:S(2)}, u32[]{:S(2)}) collective-permute-start(f32[131,128]{1,0:T(8,128)S(1)} %pad_maximum_fusion.1), channel_id=1, source_target_pairs={{0,7},{1,8},{2,9},{3,10},{4,11},{5,12},{6,13},{7,14},{8,15},{9,16}... | collective-permute-start | bytes 201224 | tf_op jit(solution)/shard_map/ppermute | solution.py:28
  17.5 30.9 %collective-permute-start.18 = (f32[131,128]{1,0:T(8,128)S(1)}, f32[131,128]{1,0:T(8,128)S(1)}, u32[]{:S(2)}, u32[]{:S(2)}) collective-permute-start(f32[131,128]{1,0:T(8,128)S(1)} %pad_maximum_fusion.1), channel_id=1, source_target_pairs={{0,6},{1,7},{2,8},{3,9},{4,10},{5,11},{6,12},{7,13},{8,14},{9,15},... | collective-permute-start | bytes 201224 | tf_op jit(solution)/shard_map/ppermute | solution.py:28
  23.5 27.3 %collective-permute-start.19 = (f32[131,128]{1,0:T(8,128)S(1)}, f32[131,128]{1,0:T(8,128)S(1)}, u32[]{:S(2)}, u32[]{:S(2)}) collective-permute-start(f32[131,128]{1,0:T(8,128)S(1)} %pad_maximum_fusion.1), channel_id=1, source_target_pairs={{0,5},{1,6},{2,7},{3,8},{4,9},{5,10},{6,11},{7,12},{8,13},{9,14},{... | collective-permute-start | bytes 201224 | tf_op jit(solution)/shard_map/ppermute | solution.py:28
  28.7 11.4 %collective-permute-start.32 = (f32[128,128]{1,0:T(8,128)S(1)}, f32[128,128]{1,0:T(8,128)S(1)}, u32[]{:S(2)}, u32[]{:S(2)}) collective-permute-start(f32[128,128]{1,0:T(8,128)S(1)} %convolution_bitcast_fusion.4), channel_id=1, source_target_pairs={{0,1},{1,0},{2,3},{3,2},{4,5},{5,4},{6,7},{7,6},{8,9},{9,8},{10,11... | collective-permute-start | bytes 196616 | tf_op jit(solution)/shard_map/ppermute | solution.py:22
  40.2 18.1 %collective-permute-start.20 = (f32[131,128]{1,0:T(8,128)S(1)}, f32[131,128]{1,0:T(8,128)S(1)}, u32[]{:S(2)}, u32[]{:S(2)}) collective-permute-start(f32[131,128]{1,0:T(8,128)S(1)} %pad_maximum_fusion.1), channel_id=1, source_target_pairs={{0,4},{1,5},{2,6},{3,7},{4,8},{5,9},{6,10},{7,11},{8,12},{9,13},{1... | collective-permute-start | bytes 201224 | tf_op jit(solution)/shard_map/ppermute | solution.py:28
  43.9 17.7 %collective-permute-start.21 = (f32[131,128]{1,0:T(8,128)S(1)}, f32[131,128]{1,0:T(8,128)S(1)}, u32[]{:S(2)}, u32[]{:S(2)}) collective-permute-start(f32[131,128]{1,0:T(8,128)S(1)} %pad_maximum_fusion.1), channel_id=1, source_target_pairs={{0,3},{1,4},{2,5},{3,6},{4,7},{5,8},{6,9},{7,10},{8,11},{9,12},{10... | collective-permute-start | bytes 201224 | tf_op jit(solution)/shard_map/ppermute | solution.py:28
  45.8 18.7 %collective-permute-start.22 = (f32[131,128]{1,0:T(8,128)S(1)}, f32[131,128]{1,0:T(8,128)S(1)}, u32[]{:S(2)}, u32[]{:S(2)}) collective-permute-start(f32[131,128]{1,0:T(8,128)S(1)} %pad_maximum_fusion.1), channel_id=1, source_target_pairs={{0,2},{1,3},{2,4},{3,5},{4,6},{5,7},{6,8},{7,9},{8,10},{9,11},{10,... | collective-permute-start | bytes 201224 | tf_op jit(solution)/shard_map/ppermute | solution.py:28
  48.5 20.7 %collective-permute-start.23 = (f32[131,128]{1,0:T(8,128)S(1)}, f32[131,128]{1,0:T(8,128)S(1)}, u32[]{:S(2)}, u32[]{:S(2)}) collective-permute-start(f32[131,128]{1,0:T(8,128)S(1)} %pad_maximum_fusion.1), channel_id=1, source_target_pairs={{0,1},{1,2},{2,3},{3,4},{4,5},{5,6},{6,7},{7,8},{8,9},{9,10},{10,1... | collective-permute-start | bytes 201224 | tf_op jit(solution)/shard_map/ppermute | solution.py:28
  50.8 22.5 %collective-permute-start.24 = (f32[131,128]{1,0:T(8,128)S(1)}, f32[131,128]{1,0:T(8,128)S(1)}, u32[]{:S(2)}, u32[]{:S(2)}) collective-permute-start(f32[131,128]{1,0:T(8,128)S(1)} %pad_maximum_fusion.1), channel_id=1, source_target_pairs={{1,0},{2,1},{3,2},{4,3},{5,4},{6,5},{7,6},{8,7},{9,8},{10,9},{11,1... | collective-permute-start | bytes 201224 | tf_op jit(solution)/shard_map/ppermute | solution.py:28
  58.3 19.0 %collective-permute-start.25 = (f32[131,128]{1,0:T(8,128)S(1)}, f32[131,128]{1,0:T(8,128)S(1)}, u32[]{:S(2)}, u32[]{:S(2)}) collective-permute-start(f32[131,128]{1,0:T(8,128)S(1)} %pad_maximum_fusion.1), channel_id=1, source_target_pairs={{2,0},{3,1},{4,2},{5,3},{6,4},{7,5},{8,6},{9,7},{10,8},{11,9},{12,... | collective-permute-start | bytes 201224 | tf_op jit(solution)/shard_map/ppermute | solution.py:28
  61.6 18.0 %collective-permute-start.26 = (f32[131,128]{1,0:T(8,128)S(1)}, f32[131,128]{1,0:T(8,128)S(1)}, u32[]{:S(2)}, u32[]{:S(2)}) collective-permute-start(f32[131,128]{1,0:T(8,128)S(1)} %pad_maximum_fusion.1), channel_id=1, source_target_pairs={{3,0},{4,1},{5,2},{6,3},{7,4},{8,5},{9,6},{10,7},{11,8},{12,9},{13... | collective-permute-start | bytes 201224 | tf_op jit(solution)/shard_map/ppermute | solution.py:28
  64.6 20.8 %collective-permute-start.27 = (f32[131,128]{1,0:T(8,128)S(1)}, f32[131,128]{1,0:T(8,128)S(1)}, u32[]{:S(2)}, u32[]{:S(2)}) collective-permute-start(f32[131,128]{1,0:T(8,128)S(1)} %pad_maximum_fusion.1), channel_id=1, source_target_pairs={{4,0},{5,1},{6,2},{7,3},{8,4},{9,5},{10,6},{11,7},{12,8},{13,9},{1... | collective-permute-start | bytes 201224 | tf_op jit(solution)/shard_map/ppermute | solution.py:28
  69.2 18.6 %collective-permute-start.28 = (f32[131,128]{1,0:T(8,128)S(1)}, f32[131,128]{1,0:T(8,128)S(1)}, u32[]{:S(2)}, u32[]{:S(2)}) collective-permute-start(f32[131,128]{1,0:T(8,128)S(1)} %pad_maximum_fusion.1), channel_id=1, source_target_pairs={{5,0},{6,1},{7,2},{8,3},{9,4},{10,5},{11,6},{12,7},{13,8},{14,9},{... | collective-permute-start | bytes 201224 | tf_op jit(solution)/shard_map/ppermute | solution.py:28
  73.3 16.7 %collective-permute-start.29 = (f32[131,128]{1,0:T(8,128)S(1)}, f32[131,128]{1,0:T(8,128)S(1)}, u32[]{:S(2)}, u32[]{:S(2)}) collective-permute-start(f32[131,128]{1,0:T(8,128)S(1)} %pad_maximum_fusion.1), channel_id=1, source_target_pairs={{6,0},{7,1},{8,2},{9,3},{10,4},{11,5},{12,6},{13,7},{14,8},{15,9},... | collective-permute-start | bytes 201224 | tf_op jit(solution)/shard_map/ppermute | solution.py:28
  77.3 16.8 %collective-permute-start.30 = (f32[131,128]{1,0:T(8,128)S(1)}, f32[131,128]{1,0:T(8,128)S(1)}, u32[]{:S(2)}, u32[]{:S(2)}) collective-permute-start(f32[131,128]{1,0:T(8,128)S(1)} %pad_maximum_fusion.1), channel_id=1, source_target_pairs={{7,0},{8,1},{9,2},{10,3},{11,4},{12,5},{13,6},{14,7},{15,8},{16,9}... | collective-permute-start | bytes 201224 | tf_op jit(solution)/shard_map/ppermute | solution.py:28
  79.6 22.1 %collective-permute-start.31 = (f32[131,128]{1,0:T(8,128)S(1)}, f32[131,128]{1,0:T(8,128)S(1)}, u32[]{:S(2)}, u32[]{:S(2)}) collective-permute-start(f32[131,128]{1,0:T(8,128)S(1)} %pad_maximum_fusion.1), channel_id=1, source_target_pairs={{8,0},{9,1},{10,2},{11,3},{12,4},{13,5},{14,6},{15,7},{16,8},{17,9... | collective-permute-start | bytes 201224 | tf_op jit(solution)/shard_map/ppermute | solution.py:28
  85.3 211.3 %collective-permute-start.6 = (f32[524,128]{1,0:T(8,128)S(1)}, f32[524,128]{1,0:T(8,128)S(1)}, u32[]{:S(2)}, u32[]{:S(2)}) collective-permute-start(f32[524,128]{1,0:T(8,128)S(1)} %pad_maximum_fusion), channel_id=1, source_target_pairs={{0,2},{1,3},{2,4},{3,5},{4,6},{5,7},{6,8},{7,9},{8,10},{9,11},{10,... | collective-permute-start | bytes 804872 | tf_op jit(solution)/shard_map/ppermute | solution.py:28
  87.7 211.7 %collective-permute-start.5 = (f32[524,128]{1,0:T(8,128)S(1)}, f32[524,128]{1,0:T(8,128)S(1)}, u32[]{:S(2)}, u32[]{:S(2)}) collective-permute-start(f32[524,128]{1,0:T(8,128)S(1)} %pad_maximum_fusion), channel_id=1, source_target_pairs={{0,3},{1,4},{2,5},{3,6},{4,7},{5,8},{6,9},{7,10},{8,11},{9,12},{10... | collective-permute-start | bytes 804872 | tf_op jit(solution)/shard_map/ppermute | solution.py:28
  90.0 213.7 %collective-permute-start.4 = (f32[524,128]{1,0:T(8,128)S(1)}, f32[524,128]{1,0:T(8,128)}, u32[]{:S(2)}, u32[]{:S(2)}) collective-permute-start(f32[524,128]{1,0:T(8,128)S(1)} %pad_maximum_fusion), channel_id=1, source_target_pairs={{0,4},{1,5},{2,6},{3,7},{4,8},{5,9},{6,10},{7,11},{8,12},{9,13},{1... | collective-permute-start | bytes 804872 | tf_op jit(solution)/shard_map/ppermute | solution.py:28
  94.1 22.4 %collective-permute-start.33 = (f32[128,128]{1,0:T(8,128)S(1)}, f32[128,128]{1,0:T(8,128)S(1)}, u32[]{:S(2)}, u32[]{:S(2)}) collective-permute-start(f32[128,128]{1,0:T(8,128)S(1)} %add.560), channel_id=1, source_target_pairs={{0,8},{1,9},{2,10},{3,11},{4,12},{5,13},{6,14},{7,15},{8,16},{9,17... | collective-permute-start | bytes 196616 | tf_op jit(solution)/shard_map/ppermute | solution.py:28
  101.7 23.7 %collective-permute-start.34 = (f32[128,128]{1,0:T(8,128)S(1)}, f32[128,128]{1,0:T(8,128)S(1)}, u32[]{:S(2)}, u32[]{:S(2)}) collective-permute-start(f32[128,128]{1,0:T(8,128)S(1)} %add.560), channel_id=1, source_target_pairs={{0,6},{1,7},{2,8},{3,9},{4,10},{5,11},{6,12},{7,13},{8,14},{9,15},... | collective-permute-start | bytes 196616 | tf_op jit(solution)/shard_map/ppermute | solution.py:28
  116.5 22.0 %collective-permute-start.35 = (f32[128,128]{1,0:T(8,128)S(1)}, f32[128,128]{1,0:T(8,128)S(1)}, u32[]{:S(2)}, u32[]{:S(2)}) collective-permute-start(f32[128,128]{1,0:T(8,128)S(1)} %add.560), channel_id=1, source_target_pairs={{0,4},{1,5},{2,6},{3,7},{4,8},{5,9},{6,10},{7,11},{8,12},{9,13},{1... | collective-permute-start | bytes 196616 | tf_op jit(solution)/shard_map/ppermute | solution.py:28
  125.4 15.3 %collective-permute-start.36 = (f32[128,128]{1,0:T(8,128)S(1)}, f32[128,128]{1,0:T(8,128)S(1)}, u32[]{:S(2)}, u32[]{:S(2)}) collective-permute-start(f32[128,128]{1,0:T(8,128)S(1)} %add.560), channel_id=1, source_target_pairs={{0,2},{1,3},{2,4},{3,5},{4,6},{5,7},{6,8},{7,9},{8,10},{9,11},{10,... | collective-permute-start | bytes 196616 | tf_op jit(solution)/shard_map/ppermute | solution.py:28
  138.5 7.2 %collective-permute-start.37 = (f32[128,128]{1,0:T(8,128)S(1)}, f32[128,128]{1,0:T(8,128)S(1)}, u32[]{:S(2)}, u32[]{:S(2)}) collective-permute-start(f32[128,128]{1,0:T(8,128)S(1)} %add.560), channel_id=1, source_target_pairs={{2,0},{3,1},{4,2},{5,3},{6,4},{7,5},{8,6},{9,7},{10,8},{11,9},{12,... | collective-permute-start | bytes 196616 | tf_op jit(solution)/shard_map/ppermute | solution.py:28
  140.6 8.3 %collective-permute-start.38 = (f32[128,128]{1,0:T(8,128)S(1)}, f32[128,128]{1,0:T(8,128)S(1)}, u32[]{:S(2)}, u32[]{:S(2)}) collective-permute-start(f32[128,128]{1,0:T(8,128)S(1)} %add.560), channel_id=1, source_target_pairs={{4,0},{5,1},{6,2},{7,3},{8,4},{9,5},{10,6},{11,7},{12,8},{13,9},{1... | collective-permute-start | bytes 196616 | tf_op jit(solution)/shard_map/ppermute | solution.py:28
  145.8 10.4 %collective-permute-start.39 = (f32[128,128]{1,0:T(8,128)S(1)}, f32[128,128]{1,0:T(8,128)S(1)}, u32[]{:S(2)}, u32[]{:S(2)}) collective-permute-start(f32[128,128]{1,0:T(8,128)S(1)} %add.560), channel_id=1, source_target_pairs={{6,0},{7,1},{8,2},{9,3},{10,4},{11,5},{12,6},{13,7},{14,8},{15,9},... | collective-permute-start | bytes 196616 | tf_op jit(solution)/shard_map/ppermute | solution.py:28
  148.9 14.4 %collective-permute-start.40 = (f32[128,128]{1,0:T(8,128)S(1)}, f32[128,128]{1,0:T(8,128)S(1)}, u32[]{:S(2)}, u32[]{:S(2)}) collective-permute-start(f32[128,128]{1,0:T(8,128)S(1)} %add.560), channel_id=1, source_target_pairs={{8,0},{9,1},{10,2},{11,3},{12,4},{13,5},{14,6},{15,7},{16,8},{17,9... | collective-permute-start | bytes 196616 | tf_op jit(solution)/shard_map/ppermute | solution.py:28
  156.1 3.1 collective-permute-start.41
  159.3 147.1 %collective-permute-start.3 = (f32[524,128]{1,0:T(8,128)S(1)}, f32[524,128]{1,0:T(8,128)S(1)}, u32[]{:S(2)}, u32[]{:S(2)}) collective-permute-start(f32[524,128]{1,0:T(8,128)S(1)} %pad_maximum_fusion), channel_id=1, source_target_pairs={{0,5},{1,6},{2,7},{3,8},{4,9},{5,10},{6,11},{7,12},{8,13},{9,14},{... | collective-permute-start | bytes 804872 | tf_op jit(solution)/shard_map/ppermute | solution.py:28
  163.3 12.4 %collective-permute-start.42 = (f32[128,128]{1,0:T(8,128)S(1)}, f32[128,128]{1,0:T(8,128)S(1)}, u32[]{:S(2)}, u32[]{:S(2)}) collective-permute-start(f32[128,128]{1,0:T(8,128)S(1)} %add.571), channel_id=1, source_target_pairs={{0,2},{1,3},{2,0},{3,1},{4,6},{5,7},{6,4},{7,5},{8,10},{9,11},{10,... | collective-permute-start | bytes 196616 | tf_op jit(solution)/shard_map/ppermute | solution.py:22
  175.8 18.1 %collective-permute-start.43 = (f32[128,128]{1,0:T(8,128)S(1)}, f32[128,128]{1,0:T(8,128)S(1)}, u32[]{:S(2)}, u32[]{:S(2)}) collective-permute-start(f32[128,128]{1,0:T(8,128)S(1)} %add.572), channel_id=1, source_target_pairs={{0,16},{1,17},{2,18},{3,19},{4,20},{5,21},{6,22},{7,23},{8,24},{9,... | collective-permute-start | bytes 196616 | tf_op jit(solution)/shard_map/ppermute | solution.py:28
  193.8 16.7 %collective-permute-start.44 = (f32[128,128]{1,0:T(8,128)S(1)}, f32[128,128]{1,0:T(8,128)S(1)}, u32[]{:S(2)}, u32[]{:S(2)}) collective-permute-start(f32[128,128]{1,0:T(8,128)S(1)} %add.572), channel_id=1, source_target_pairs={{0,12},{1,13},{2,14},{3,15},{4,16},{5,17},{6,18},{7,19},{8,20},{9,... | collective-permute-start | bytes 196616 | tf_op jit(solution)/shard_map/ppermute | solution.py:28
  210.6 15.1 %collective-permute-start.45 = (f32[128,128]{1,0:T(8,128)S(1)}, f32[128,128]{1,0:T(8,128)S(1)}, u32[]{:S(2)}, u32[]{:S(2)}) collective-permute-start(f32[128,128]{1,0:T(8,128)S(1)} %add.572), channel_id=1, source_target_pairs={{0,8},{1,9},{2,10},{3,11},{4,12},{5,13},{6,14},{7,15},{8,16},{9,17... | collective-permute-start | bytes 196616 | tf_op jit(solution)/shard_map/ppermute | solution.py:28
  225.7 11.3 %collective-permute-start.46 = (f32[128,128]{1,0:T(8,128)S(1)}, f32[128,128]{1,0:T(8,128)S(1)}, u32[]{:S(2)}, u32[]{:S(2)}) collective-permute-start(f32[128,128]{1,0:T(8,128)S(1)} %add.572), channel_id=1, source_target_pairs={{0,4},{1,5},{2,6},{3,7},{4,8},{5,9},{6,10},{7,11},{8,12},{9,13},{1... | collective-permute-start | bytes 196616 | tf_op jit(solution)/shard_map/ppermute | solution.py:28
  237.0 7.0 %collective-permute-start.47 = (f32[128,128]{1,0:T(8,128)S(1)}, f32[128,128]{1,0:T(8,128)S(1)}, u32[]{:S(2)}, u32[]{:S(2)}) collective-permute-start(f32[128,128]{1,0:T(8,128)S(1)} %add.572), channel_id=1, source_target_pairs={{4,0},{5,1},{6,2},{7,3},{8,4},{9,5},{10,6},{11,7},{12,8},{13,9},{1... | collective-permute-start | bytes 196616 | tf_op jit(solution)/shard_map/ppermute | solution.py:28
  244.0 11.0 %collective-permute-start.48 = (f32[128,128]{1,0:T(8,128)S(1)}, f32[128,128]{1,0:T(8,128)S(1)}, u32[]{:S(2)}, u32[]{:S(2)}) collective-permute-start(f32[128,128]{1,0:T(8,128)S(1)} %add.572), channel_id=1, source_target_pairs={{8,0},{9,1},{10,2},{11,3},{12,4},{13,5},{14,6},{15,7},{16,8},{17,9... | collective-permute-start | bytes 196616 | tf_op jit(solution)/shard_map/ppermute | solution.py:28
  255.0 15.8 %collective-permute-start.49 = (f32[128,128]{1,0:T(8,128)S(1)}, f32[128,128]{1,0:T(8,128)S(1)}, u32[]{:S(2)}, u32[]{:S(2)}) collective-permute-start(f32[128,128]{1,0:T(8,128)S(1)} %add.572), channel_id=1, source_target_pairs={{12,0},{13,1},{14,2},{15,3},{16,4},{17,5},{18,6},{19,7},{20,8},{21... | collective-permute-start | bytes 196616 | tf_op jit(solution)/shard_map/ppermute | solution.py:28
  270.8 15.0 %collective-permute-start.50 = (f32[128,128]{1,0:T(8,128)S(1)}, f32[128,128]{1,0:T(8,128)S(1)}, u32[]{:S(2)}, u32[]{:S(2)}) collective-permute-start(f32[128,128]{1,0:T(8,128)S(1)} %add.572), channel_id=1, source_target_pairs={{16,0},{17,1},{18,2},{19,3},{20,4},{21,5},{22,6},{23,7},{24,8},{25... | collective-permute-start | bytes 196616 | tf_op jit(solution)/shard_map/ppermute | solution.py:28
  285.8 3.1 collective-permute-start.51
  289.0 33.2 %collective-permute-start.2 = (f32[524,128]{1,0:T(8,128)S(1)}, f32[524,128]{1,0:T(8,128)S(1)}, u32[]{:S(2)}, u32[]{:S(2)}) collective-permute-start(f32[524,128]{1,0:T(8,128)S(1)} %pad_maximum_fusion), channel_id=1, source_target_pairs={{0,6},{1,7},{2,8},{3,9},{4,10},{5,11},{6,12},{7,13},{8,14},{9,15},... | collective-permute-start | bytes 804872 | tf_op jit(solution)/shard_map/ppermute | solution.py:28
  296.7 67.4 %collective-permute-start.1 = (f32[524,128]{1,0:T(8,128)S(1)}, f32[524,128]{1,0:T(8,128)S(1)}, u32[]{:S(2)}, u32[]{:S(2)}) collective-permute-start(f32[524,128]{1,0:T(8,128)S(1)} %pad_maximum_fusion), channel_id=1, source_target_pairs={{0,7},{1,8},{2,9},{3,10},{4,11},{5,12},{6,13},{7,14},{8,15},{9,16}... | collective-permute-start | bytes 804872 | tf_op jit(solution)/shard_map/ppermute | solution.py:28
  299.4 66.6 %collective-permute-start.7 = (f32[524,128]{1,0:T(8,128)S(1)}, f32[524,128]{1,0:T(8,128)S(1)}, u32[]{:S(2)}, u32[]{:S(2)}) collective-permute-start(f32[524,128]{1,0:T(8,128)S(1)} %pad_maximum_fusion), channel_id=1, source_target_pairs={{0,1},{1,2},{2,3},{3,4},{4,5},{5,6},{6,7},{7,8},{8,9},{9,10},{10,1... | collective-permute-start | bytes 804872 | tf_op jit(solution)/shard_map/ppermute | solution.py:28
  303.6 66.9 %collective-permute-start = (f32[524,128]{1,0:T(8,128)S(1)}, f32[524,128]{1,0:T(8,128)S(1)}, u32[]{:S(2)}, u32[]{:S(2)}) collective-permute-start(f32[524,128]{1,0:T(8,128)S(1)} %pad_maximum_fusion), channel_id=1, source_target_pairs={{0,8},{1,9},{2,10},{3,11},{4,12},{5,13},{6,14},{7,15},{8,16},{9,17... | collective-permute-start | bytes 804872 | tf_op jit(solution)/shard_map/ppermute | solution.py:28
  306.4 66.0 %collective-permute-start.15 = (f32[524,128]{1,0:T(8,128)S(1)}, f32[524,128]{1,0:T(8,128)S(1)}, u32[]{:S(2)}, u32[]{:S(2)}) collective-permute-start(f32[524,128]{1,0:T(8,128)S(1)} %pad_maximum_fusion), channel_id=1, source_target_pairs={{8,0},{9,1},{10,2},{11,3},{12,4},{13,5},{14,6},{15,7},{16,8},{17,9... | collective-permute-start | bytes 804872 | tf_op jit(solution)/shard_map/ppermute | solution.py:28
  322.1 74.0 %collective-permute-start.14 = (f32[524,128]{1,0:T(8,128)S(1)}, f32[524,128]{1,0:T(8,128)S(1)}, u32[]{:S(2)}, u32[]{:S(2)}) collective-permute-start(f32[524,128]{1,0:T(8,128)S(1)} %pad_maximum_fusion), channel_id=1, source_target_pairs={{7,0},{8,1},{9,2},{10,3},{11,4},{12,5},{13,6},{14,7},{15,8},{16,9}... | collective-permute-start | bytes 804872 | tf_op jit(solution)/shard_map/ppermute | solution.py:28
  364.1 53.3 %collective-permute-start.13 = (f32[524,128]{1,0:T(8,128)S(1)}, f32[524,128]{1,0:T(8,128)S(1)}, u32[]{:S(2)}, u32[]{:S(2)}) collective-permute-start(f32[524,128]{1,0:T(8,128)S(1)} %pad_maximum_fusion), channel_id=1, source_target_pairs={{6,0},{7,1},{8,2},{9,3},{10,4},{11,5},{12,6},{13,7},{14,8},{15,9},... | collective-permute-start | bytes 804872 | tf_op jit(solution)/shard_map/ppermute | solution.py:28
  366.0 72.6 %collective-permute-start.12 = (f32[524,128]{1,0:T(8,128)S(1)}, f32[524,128]{1,0:T(8,128)S(1)}, u32[]{:S(2)}, u32[]{:S(2)}) collective-permute-start(f32[524,128]{1,0:T(8,128)S(1)} %pad_maximum_fusion), channel_id=1, source_target_pairs={{5,0},{6,1},{7,2},{8,3},{9,4},{10,5},{11,6},{12,7},{13,8},{14,9},{... | collective-permute-start | bytes 804872 | tf_op jit(solution)/shard_map/ppermute | solution.py:28
  370.5 90.2 %collective-permute-start.11 = (f32[524,128]{1,0:T(8,128)S(1)}, f32[524,128]{1,0:T(8,128)S(1)}, u32[]{:S(2)}, u32[]{:S(2)}) collective-permute-start(f32[524,128]{1,0:T(8,128)S(1)} %pad_maximum_fusion), channel_id=1, source_target_pairs={{4,0},{5,1},{6,2},{7,3},{8,4},{9,5},{10,6},{11,7},{12,8},{13,9},{1... | collective-permute-start | bytes 804872 | tf_op jit(solution)/shard_map/ppermute | solution.py:28
  372.5 104.0 %collective-permute-start.10 = (f32[524,128]{1,0:T(8,128)S(1)}, f32[524,128]{1,0:T(8,128)S(1)}, u32[]{:S(2)}, u32[]{:S(2)}) collective-permute-start(f32[524,128]{1,0:T(8,128)S(1)} %pad_maximum_fusion), channel_id=1, source_target_pairs={{3,0},{4,1},{5,2},{6,3},{7,4},{8,5},{9,6},{10,7},{11,8},{12,9},{13... | collective-permute-start | bytes 804872 | tf_op jit(solution)/shard_map/ppermute | solution.py:28
  396.2 16.9 %collective-permute-start.52 = (f32[128,128]{0,1:T(8,128)S(1)}, f32[128,128]{0,1:T(8,128)S(1)}, u32[]{:S(2)}, u32[]{:S(2)}) collective-permute-start(f32[128,128]{0,1:T(8,128)S(1)} %add.585), channel_id=1, source_target_pairs={{0,2},{1,3},{2,0},{3,1},{4,6},{5,7},{6,4},{7,5},{8,10},{9,11},{10,... | collective-permute-start | bytes 196616 | tf_op jit(solution)/shard_map/ppermute | solution.py:22
  413.0 87.9 %collective-permute-start.9 = (f32[524,128]{1,0:T(8,128)S(1)}, f32[524,128]{1,0:T(8,128)S(1)}, u32[]{:S(2)}, u32[]{:S(2)}) collective-permute-start(f32[524,128]{1,0:T(8,128)S(1)} %pad_maximum_fusion), channel_id=1, source_target_pairs={{2,0},{3,1},{4,2},{5,3},{6,4},{7,5},{8,6},{9,7},{10,8},{11,9},{12,... | collective-permute-start | bytes 804872 | tf_op jit(solution)/shard_map/ppermute | solution.py:28
  417.4 7.7 %collective-permute-start.53 = (f32[128,128]{0,1:T(8,128)S(1)}, f32[128,128]{0,1:T(8,128)S(1)}, u32[]{:S(2)}, u32[]{:S(2)}) collective-permute-start(f32[128,128]{0,1:T(8,128)S(1)} %add.586), channel_id=1, source_target_pairs={{0,4},{1,5},{2,6},{3,7},{4,0},{5,1},{6,2},{7,3},{8,12},{9,13},{10,... | collective-permute-start | bytes 196616 | tf_op jit(solution)/shard_map/ppermute | solution.py:22
  425.1 9.4 %collective-permute-start.54 = (f32[1,128,16]{1,2,0:T(8,128)S(1)}, f32[1,128,16]{1,2,0:T(8,128)S(1)}, u32[]{:S(2)}, u32[]{:S(2)}) collective-permute-start(f32[1,128,16]{1,2,0:T(8,128)S(1)} %fusion.466), channel_id=1, source_target_pairs={{0,8},{1,9},{2,10},{3,11},{4,12},{5,13},{6,14},{7,15},{8,0},{9,1},... | collective-permute-start | bytes 24584 | tf_op jit(solution)/shard_map/ppermute | solution.py:22
  434.6 75.2 %collective-permute-start.8 = (f32[524,128]{1,0:T(8,128)S(1)}, f32[524,128]{1,0:T(8,128)S(1)}, u32[]{:S(2)}, u32[]{:S(2)}) collective-permute-start(f32[524,128]{1,0:T(8,128)S(1)} %pad_maximum_fusion), channel_id=1, source_target_pairs={{1,0},{2,1},{3,2},{4,3},{5,4},{6,5},{7,6},{8,7},{9,8},{10,9},{11,1... | collective-permute-start | bytes 804872 | tf_op jit(solution)/shard_map/ppermute | solution.py:28
  438.7 14.3 %collective-permute-start.55 = (f32[2,128,16]{1,2,0:T(8,128)S(1)}, f32[2,128,16]{1,2,0:T(8,128)S(1)}, u32[]{:S(2)}, u32[]{:S(2)}) collective-permute-start(f32[2,128,16]{1,2,0:T(8,128)S(1)} %maximum_select_fusion.10), channel_id=1, source_target_pairs={{0,16},{1,17},{2,18},{3,19},{4,20},{5,21},{6,22},{7,23},{8,24},{9,... | collective-permute-start | bytes 49160 | tf_op jit(solution)/shard_map/ppermute | solution.py:22
  453.0 5.8 %collective-permute-start.56 = (f32[4,128,16]{1,2,0:T(8,128)S(1)}, f32[4,128,16]{1,2,0:T(8,128)S(1)}, u32[]{:S(2)}, u32[]{:S(2)}) collective-permute-start(f32[4,128,16]{1,2,0:T(8,128)S(1)} %maximum_select_fusion.8), channel_id=1, source_target_pairs={{0,32},{1,33},{2,34},{3,35},{4,36},{5,37},{6,38},{7,39},{8,40},{9,... | collective-permute-start | bytes 98312 | tf_op jit(solution)/shard_map/ppermute | solution.py:22
  458.8 7.7 %collective-permute-start.57 = (f32[8,128,16]{1,2,0:T(8,128)S(1)}, f32[8,128,16]{1,2,0:T(8,128)S(1)}, u32[]{:S(2)}, u32[]{:S(2)}) collective-permute-start(f32[8,128,16]{1,2,0:T(8,128)S(1)} %maximum_select_fusion.3), channel_id=1, source_target_pairs={{0,64},{1,65},{2,66},{3,67},{4,68},{5,69},{6,70},{7,71},{8,72},{9,... | collective-permute-start | bytes 196616 | tf_op jit(solution)/shard_map/ppermute | solution.py:22
  466.5 6.9 %collective-permute-start.58 = (f32[16,128,16]{1,2,0:T(8,128)S(1)}, f32[16,128,16]{1,2,0:T(8,128)S(1)}, u32[]{:S(2)}, u32[]{:S(2)}) collective-permute-start(f32[16,128,16]{1,2,0:T(8,128)S(1)} %maximum_select_fusion.2), channel_id=1, source_target_pairs={{0,128},{1,129},{2,130},{3,131},{4,132},{5,133},{6,134},{7,135},{8... | collective-permute-start | bytes 393224 | tf_op jit(solution)/shard_map/ppermute | solution.py:22
  473.4 9.8 %collective-permute-start.59 = (f32[32,128,16]{1,2,0:T(8,128)S(1)}, f32[32,128,16]{1,2,0:T(8,128)S(1)}, u32[]{:S(2)}, u32[]{:S(2)}) collective-permute-start(f32[32,128,16]{1,2,0:T(8,128)S(1)} %maximum_select_fusion.1), channel_id=1, source_target_pairs={{0,256},{1,257},{2,258},{3,259},{4,260},{5,261},{6,262},{7,263},{8... | collective-permute-start | bytes 786440 | tf_op jit(solution)/shard_map/ppermute | solution.py:22
  498.7 3.1 collective-permute-start.60
  501.8 5.8 %collective-permute-start.61 = (f32[64,128]{1,0:T(8,128)S(1)}, f32[64,128]{1,0:T(8,128)S(1)}, u32[]{:S(2)}, u32[]{:S(2)}) collective-permute-start(f32[64,128]{1,0:T(8,128)S(1)} %maximum_select_fusion.9), channel_id=1, source_target_pairs={{0,2},{1,3},{2,0},{3,1},{4,6},{5,7},{6,4},{7,5},{8,10},{9,11},{10,... | collective-permute-start | bytes 98312 | tf_op jit(solution)/shard_map/ppermute | solution.py:22
  507.8 3.1 collective-permute-start.62
  (20 other events, 372.5 us)
